TPU v7x, 32 devices: a whole 2x2x4 slice. The times are simulated.
32 devices in a mesh: dp: 4 (over y, x), seq: 2 (over core), tensor: 4 (over z).
Axes of the slice: x: 2, y: 2, z: 4, core: 2. Of those that a mesh axis runs over, the one named last changes fastest.
Arguments:
- x_in: bfloat16 [4, 1024, 8192], P('dp', 'seq', 'tensor'), may hold values from -0.0625 to 0.0625
- b_in: bfloat16 [4, 1024, 1024], P('dp', 'seq', 'tensor'), may hold values from -3 to 3
- c_in: bfloat16 [4, 1024, 1024], P('dp', 'seq', 'tensor'), may hold values from -3 to 3
- log_decay: float32 [4, 1024, 128], P('dp', 'seq', 'tensor'), may hold values from -1 to 0, as said below
- out_weight: bfloat16 [8192, 4096], P('tensor'), may hold values from -0.0625 to 0.0625
- out_grad: bfloat16 [4, 1024, 4096], P('dp', 'seq', 'tensor'), may hold values from -0.078125 to 0.078125
Outputs:
- weight_grad: bfloat16 [8192, 4096], P('tensor', ('dp', 'seq'))
- x_grad: bfloat16 [4, 1024, 8192], P('dp', 'seq', 'tensor')
- b_grad: bfloat16 [4, 1024, 1024], P('dp', 'seq', 'tensor')
- c_grad: bfloat16 [4, 1024, 1024], P('dp', 'seq', 'tensor')
Inputs may be any that keep to these rules, and one draw needn't show every extreme that they name: `log_decay`: every log-decay is below zero.
All inputs are finite; a program needn't handle non-finite values.
Results may differ from a plain program's by a relative error of at most 0.017.
Values may be sent and summed in bfloat16 or wider, within the bound.
No kernel may reach another device: no remote copies, remote signals or barrier semaphores. Data moves between devices by JAX's collectives and lax.ppermute only.
A program may use at most 192 MiB of HBM per device.

v0:
```python
import functools

import jax
import jax.numpy as jnp
from jax import lax
from jax.experimental import pallas as pl
from jax.experimental.pallas import tpu as pltpu
from jax.sharding import PartitionSpec as P

HEAD_DIM = 64
STATE = 128
CHUNK = 128
LANES = 128
PARTS = 1

BF16 = jnp.bfloat16
F32 = jnp.float32


def dot(a, b, dims):
    return lax.dot_general(a, b, (dims, ((), ())), preferred_element_type=F32)


NN = ((1,), (0,))
NT = ((1,), (1,))
TN = ((0,), (0,))


def causal_mask():
    rows = lax.broadcasted_iota(jnp.int32, (CHUNK, CHUNK), 0)
    cols = lax.broadcasted_iota(jnp.int32, (CHUNK, CHUNK), 1)
    return rows >= cols


def chunk_decays(decays):
    ones = jnp.where(causal_mask(), 1.0, 0.0).astype(BF16)
    first = decays.astype(BF16)
    rest = decays - first.astype(F32)
    second = rest.astype(BF16)
    third = (rest - second.astype(F32)).astype(BF16)
    running = dot(ones, first, NN) + dot(ones, second, NN) + dot(ones, third, NN)
    half = 0.5 * running[CHUNK - 1 : CHUNK, :]
    return jnp.exp(running - half), jnp.exp(half - running), jnp.exp(half)


def over_columns(factors, block):
    rows = factors.shape[0]
    per_block = LANES // HEAD_DIM
    lanes = lax.broadcasted_iota(jnp.int32, (rows, LANES), 1)
    head = block * per_block
    return jnp.where(
        lanes < HEAD_DIM,
        jnp.broadcast_to(factors[:, head : head + 1], (rows, LANES)),
        jnp.broadcast_to(factors[:, head + 1 : head + 2], (rows, LANES)),
    )


def over_group(factors, group, width):
    blocks = width // LANES
    return jnp.concatenate(
        [over_columns(factors, group * blocks + i) for i in range(blocks)], axis=1
    )


def states_kernel(x_ref, b_ref, decay_ref, scaled_ref, state_ref, *, groups):
    chunk = pl.program_id(0)
    width = x_ref.shape[1] // groups

    @pl.when(chunk == 0)
    def _():
        state_ref[...] = jnp.zeros_like(state_ref)

    _, shrink, half = chunk_decays(decay_ref[...])
    for g in range(groups):
        cols = slice(g * width, (g + 1) * width)
        scaled = (x_ref[:, cols].astype(F32) * over_group(shrink, g, width)).astype(BF16)
        scaled_ref[:, cols] = scaled
        writes = b_ref[:, g * STATE : (g + 1) * STATE]
        halves = over_group(half, g, width)
        rows = slice(g * STATE, (g + 1) * STATE)
        state_ref[rows, :] = halves * (halves * state_ref[rows, :] + dot(writes, scaled, TN))


def scan_kernel(
    scaled_ref, b_ref, c_ref, decay_ref, enter_ref, rows_ref, held_ref, state_ref, *, groups
):
    chunk = pl.program_id(0)
    width = scaled_ref.shape[1] // groups

    @pl.when(chunk == 0)
    def _():
        state_ref[...] = enter_ref[...]

    grow, _, half = chunk_decays(decay_ref[...])
    mask = causal_mask()
    for g in range(groups):
        cols = slice(g * width, (g + 1) * width)
        rows = slice(g * STATE, (g + 1) * STATE)
        scaled = scaled_ref[:, cols]
        writes = b_ref[:, rows]
        reads = c_ref[:, rows]
        halves = over_group(half, g, width)
        held = halves * state_ref[rows, :]
        held_low = held.astype(BF16)
        held_ref[0, rows, :] = held_low
        affinity = jnp.where(mask, dot(reads, writes, NT), 0.0).astype(BF16)
        out = dot(affinity, scaled, NN) + dot(reads, held_low, NN)
        out = out * over_group(grow, g, width)
        rows_ref[cols, :] = out.T.astype(BF16)
        state_ref[rows, :] = halves * (held + dot(writes, scaled, TN))


def pulls_kernel(grad_ref, c_ref, decay_ref, scaled_ref, state_ref, *, groups):
    step = pl.program_id(0)
    width = grad_ref.shape[1] // groups

    @pl.when(step == 0)
    def _():
        state_ref[...] = jnp.zeros_like(state_ref)

    grow, _, half = chunk_decays(decay_ref[...])
    for g in range(groups):
        cols = slice(g * width, (g + 1) * width)
        rows = slice(g * STATE, (g + 1) * STATE)
        scaled = (grad_ref[:, cols].astype(F32) * over_group(grow, g, width)).astype(BF16)
        scaled_ref[:, cols] = scaled
        halves = over_group(half, g, width)
        pulled = dot(c_ref[:, rows], scaled, TN)
        state_ref[rows, :] = halves * (halves * state_ref[rows, :] + pulled)


def grads_kernel(
    grad_ref, scaled_ref, b_ref, c_ref, decay_ref, held_ref, leave_ref,
    x_grad_ref, b_grad_ref, c_grad_ref, state_ref, *, groups,
):
    step = pl.program_id(0)
    width = grad_ref.shape[1] // groups

    @pl.when(step == 0)
    def _():
        state_ref[...] = leave_ref[...]

    _, shrink, half = chunk_decays(decay_ref[...])
    mask = causal_mask()
    for g in range(groups):
        cols = slice(g * width, (g + 1) * width)
        rows = slice(g * STATE, (g + 1) * STATE)
        grad = grad_ref[:, cols]
        scaled = scaled_ref[:, cols]
        writes = b_ref[:, rows]
        reads = c_ref[:, rows]
        halves = over_group(half, g, width)
        left = halves * state_ref[rows, :]
        left_low = left.astype(BF16)
        affinity = jnp.where(mask, dot(reads, writes, NT), 0.0).astype(BF16)
        x_grad = dot(affinity, grad, TN) + dot(writes, left_low, NN)
        x_grad_ref[:, cols] = (x_grad * over_group(shrink, g, width)).astype(BF16)
        pair = jnp.where(mask, dot(grad, scaled, NT), 0.0).astype(BF16)
        c_grad = dot(pair, writes, NN) + dot(grad, held_ref[0, rows, :], NT)
        c_grad_ref[:, rows] = c_grad.astype(BF16)
        b_grad = dot(pair, reads, TN) + dot(scaled, left_low, NT)
        b_grad_ref[:, rows] = b_grad.astype(BF16)
        state_ref[rows, :] = halves * (left + dot(reads, grad, TN))


def scan_calls(tokens, heads, groups):
    inner = heads * HEAD_DIM
    width = inner // groups
    keys = groups * STATE
    chunks = tokens // CHUNK
    call = functools.partial(pl.pallas_call, grid=(chunks,))

    def ahead(cols):
        return pl.BlockSpec((CHUNK, cols), lambda i: (i, 0))

    def back(cols):
        return pl.BlockSpec((CHUNK, cols), lambda i: (chunks - 1 - i, 0))

    whole = pl.BlockSpec((keys, width), lambda i: (0, 0))
    state_type = jax.ShapeDtypeStruct((keys, width), F32)
    rows_type = jax.ShapeDtypeStruct((tokens, inner), BF16)
    keys_type = jax.ShapeDtypeStruct((tokens, keys), BF16)
    held_type = jax.ShapeDtypeStruct((chunks, keys, width), BF16)
    scratch = [pltpu.VMEM((keys, width), F32)]
    states = call(
        functools.partial(states_kernel, groups=groups),
        in_specs=[ahead(inner), ahead(keys), ahead(heads)],
        out_specs=[ahead(inner), whole],
        out_shape=[rows_type, state_type],
        name="states",
    )
    scan = call(
        functools.partial(scan_kernel, groups=groups),
        in_specs=[ahead(inner), ahead(keys), ahead(keys), ahead(heads), whole],
        out_specs=[
            pl.BlockSpec((inner, CHUNK), lambda i: (0, i)),
            pl.BlockSpec((1, keys, width), lambda i: (i, 0, 0)),
        ],
        out_shape=[jax.ShapeDtypeStruct((inner, tokens), BF16), held_type],
        scratch_shapes=scratch,
        name="scan",
    )
    pulls = call(
        functools.partial(pulls_kernel, groups=groups),
        in_specs=[back(inner), back(keys), back(heads)],
        out_specs=[back(inner), whole],
        out_shape=[rows_type, state_type],
        name="pulls",
    )
    grads = call(
        functools.partial(grads_kernel, groups=groups),
        in_specs=[
            back(inner), back(inner), back(keys), back(keys), back(heads),
            pl.BlockSpec((1, keys, width), lambda i: (chunks - 1 - i, 0, 0)), whole,
        ],
        out_specs=[back(inner), back(keys), back(keys)],
        out_shape=[rows_type, keys_type, keys_type],
        scratch_shapes=scratch,
        name="grads",
    )
    return states, scan, pulls, grads


def passed_along(shard, axis, by):
    length = lax.axis_size(axis)
    pairs = [(i, i + by) for i in range(length) if 0 <= i + by < length]
    return lax.ppermute(shard, axis, pairs)


def chained(local, log_decay, groups, axis, by):
    incoming = passed_along(local, axis, by)
    turns = lax.axis_size(axis) - 1
    if turns > 1:
        total = jnp.exp(jnp.sum(log_decay, axis=0)).reshape(groups, 1, -1)
        spread = jnp.repeat(total, HEAD_DIM, axis=2)
        spread = jnp.broadcast_to(spread, (groups, STATE, spread.shape[2]))
        spread = spread.reshape(local.shape)

        def turn(_, arrived):
            return passed_along(spread * arrived + local, axis, by)

        incoming = lax.fori_loop(0, turns - 1, turn, incoming)
    return incoming


def any_mesh(rows_t, out_grad, out_weight):
    full = lax.all_gather(out_grad, "tensor", axis=1, tiled=True)
    y_grad = lax.dot_general(
        full, out_weight, (NT, ((), ())), preferred_element_type=F32
    ).astype(BF16)
    part = lax.dot_general(rows_t, full, (NN, ((), ())), preferred_element_type=F32)
    weight_grad = lax.psum_scatter(
        part.astype(BF16), ("dp", "seq"), scatter_dimension=1, tiled=True
    )
    return y_grad, weight_grad


def project_kernel(table_ref, slots_ref, low_ref, high_ref, *refs, first, last):
    step = pl.program_id(0)
    out_ref, total_ref = refs[-2:]
    got = dot(slots_ref[0, 0], low_ref[...], NT) + dot(slots_ref[0, 1], high_ref[...], NT)

    @pl.when(step == 0)
    def _():
        total_ref[...] = got if first else refs[0][...] + got

    @pl.when(step > 0)
    def _():
        total_ref[...] += got

    @pl.when(step == pl.num_programs(0) - 1)
    def _():
        out_ref[...] = total_ref[...].astype(out_ref.dtype)


def project(table, slots, out_weight, part, parts, before):
    tokens, wide = slots.shape[2:]
    inner = out_weight.shape[0]
    first, last = before is None, part == parts - 1
    whole = pl.BlockSpec((tokens, inner), lambda i, t: (0, 0))
    return pl.pallas_call(
        functools.partial(project_kernel, first=first, last=last),
        grid_spec=pltpu.PrefetchScalarGridSpec(
            num_scalar_prefetch=1,
            grid=(4,),
            in_specs=[
                pl.BlockSpec((1, 2, tokens, wide), lambda i, t: (i, 0, 0, 0)),
                pl.BlockSpec((inner, wide), lambda i, t: (0, t[4 + i] * 2 * parts + part)),
                pl.BlockSpec((inner, wide), lambda i, t: (0, (t[4 + i] * 2 + 1) * parts + part)),
            ]
            + ([] if first else [whole]),
            out_specs=whole,
            scratch_shapes=[pltpu.VMEM((tokens, inner), F32)],
        ),
        out_shape=jax.ShapeDtypeStruct((tokens, inner), BF16 if last else F32),
        name="project",
    )(table, slots, out_weight, out_weight, *([] if first else [before]))


def partial_kernel(table_ref, own_ref, other_ref, mine_ref, theirs_ref, x_ref, y_ref):
    step = pl.program_id(0)
    got = dot(own_ref[...], mine_ref[0, 0], NN) + dot(other_ref[...], theirs_ref[0], NN)
    got = got.astype(BF16)

    @pl.when(step < 2)
    def _():
        x_ref[0] = got

    @pl.when(step >= 2)
    def _():
        y_ref[0] = got


def partials(table, own, other, slots, theirs, targets, name):
    inner, tokens = own.shape
    half = inner // 2
    wide = slots.shape[3]

    def slot(i, t):
        picked = t[targets[3]]
        for place in (2, 1, 0):
            picked = jnp.where(i == place, t[targets[place]], picked)
        return picked

    rows = pl.BlockSpec((half, tokens), lambda i, t: (i // 2, 0))
    out_type = jax.ShapeDtypeStruct((2, half, wide), BF16)
    return pl.pallas_call(
        partial_kernel,
        grid_spec=pltpu.PrefetchScalarGridSpec(
            num_scalar_prefetch=1,
            grid=(4,),
            in_specs=[
                rows,
                rows,
                pl.BlockSpec((1, 1, tokens, wide), lambda i, t: (slot(i, t), t[8], 0, 0)),
                pl.BlockSpec((1, tokens, wide), lambda i, t: (slot(i, t), 0, 0)),
            ],
            out_specs=[
                pl.BlockSpec((1, half, wide), lambda i, t: (jnp.minimum(i, 1), 0, 0)),
                pl.BlockSpec((1, half, wide), lambda i, t: (jnp.maximum(i - 2, 0), 0, 0)),
            ],
        ),
        out_shape=[out_type, out_type],
        name=name,
    )(table, own, other, slots, theirs)


def swapped(value, axis, by):
    return lax.ppermute(value, axis, [(i, i ^ by) for i in range(lax.axis_size(axis))])


def total(*terms):
    return functools.reduce(jnp.add, [t.astype(F32) for t in terms]).astype(BF16)


def gathered(own, place, after):
    own = own if after is None else lax.optimization_barrier((own, after))[0]
    up = passed_along(own, "tensor", 1)
    down = passed_along(own, "tensor", -1)
    across = swapped_across(own)
    far = lax.ppermute(across, "tensor", [(1, 0), (2, 3)])
    slots = jnp.stack(
        [own, jnp.where(place == 0, far, up), across, jnp.where(place == 3, far, down)]
    )
    return slots, across


def swapped_across(own):
    return lax.ppermute(own, "tensor", [(i, (i + 2) % 4) for i in range(4)])


def this_mesh(rows_t, out_grad, out_weight):
    tokens, features = out_grad.shape
    parts = PARTS
    wide = features // 2 // parts
    place = lax.axis_index("tensor")
    repo = lax.axis_index("dp")
    core = lax.axis_index("seq")
    table = jnp.stack(
        [(place - (repo ^ r)) % 4 for r in range(4)]
        + [(place - s) % 4 for s in range(4)]
        + [core]
    ).astype(jnp.int32)
    split = out_grad.reshape(tokens, 2, parts, wide).transpose(2, 1, 0, 3)
    other = swapped(rows_t, "seq", 1)
    y_grad = None
    after = None
    pieces = []
    for part in range(parts):
        slots, after = gathered(split[part], place, after)
        theirs = lax.dynamic_index_in_dim(slots, 1 - core, 1, keepdims=False)
        theirs = swapped(theirs, "seq", 1)
        x_send, y_send = partials(table, rows_t, other, slots, theirs, (1, 3, 2, 3), "sent")
        x_got = swapped(x_send, "dp", 1)
        y_got = swapped(y_send, "dp", 2)
        x_kept, y_kept = partials(table, rows_t, other, slots, theirs, (0, 2, 0, 1), "kept")
        x_last = swapped(total(x_kept[1], x_got[1]), "dp", 2)
        y_last = swapped(total(y_kept[1], y_got[1]), "dp", 1)
        pieces.append(
            jnp.concatenate(
                [total(x_kept[0], x_got[0], x_last), total(y_kept[0], y_got[0], y_last)]
            )
        )
        y_grad = project(table, slots, out_weight, part, parts, y_grad)
    return y_grad, jnp.concatenate(pieces, axis=1)


def per_device(x_in, b_in, c_in, log_decay, out_weight, out_grad):
    x_in, b_in, c_in, log_decay, out_grad = (
        x_in[0], b_in[0], c_in[0], log_decay[0], out_grad[0],
    )
    tokens, heads = log_decay.shape
    groups = b_in.shape[1] // STATE
    states, scan, pulls, grads = scan_calls(tokens, heads, groups)
    scaled, end_local = states(x_in, b_in, log_decay)
    entering = chained(end_local, log_decay, groups, "seq", 1)
    rows_t, held = scan(scaled, b_in, c_in, log_decay, entering)
    sizes = tuple(lax.axis_size(name) for name in ("dp", "seq", "tensor"))
    project_both = this_mesh if sizes == (4, 2, 4) else any_mesh
    y_grad, weight_grad = project_both(rows_t, out_grad, out_weight)
    grad, start_local = pulls(y_grad, c_in, log_decay)
    leaving = chained(start_local, log_decay, groups, "seq", -1)
    x_grad, b_grad, c_grad = grads(grad, scaled, b_in, c_in, log_decay, held, leaving)
    return weight_grad, x_grad[None], b_grad[None], c_grad[None]


def solution(mesh):
    tokens_spec = P("dp", "seq", "tensor")
    return jax.shard_map(
        per_device,
        mesh=mesh,
        in_specs=(tokens_spec,) * 4 + (P("tensor", None), tokens_spec),
        out_specs=(P("tensor", ("dp", "seq")),) + (tokens_spec,) * 3,
        check_vma=False,
    )
```

profile of v0, /device:TPU:26, one launch (start us, length us, event | category | flops | bytes accessed | tf_op | source)
XLA Modules:
  0.0 187.4 jit_solution(10919336532671593095)
XLA Ops:
  0.6 1.5 copy.12
  4.0 6.7 %states.1 = (bf16[512,2048]{1,0:T(8,128)(2,1)}, f32[256,1024]{1,0:T(8,128)}) custom-call(bf16[512,2048]{1,0:T(8,128)(2,1)} %bitcast.54, bf16[512,256]{1,0:T(8,128)(2,1)} %bitcast.48, f32[512,32]{1,0:T(8,128)} %bitcast.39), custom_call_target="tpu_custom_call" | custom-call | tf_op jit(solution)/shard_map/states/pallas_call | solution.py:415
  10.7 1.5 collective-permute-start
  12.2 3.3 %collective-permute-start.5 = (bf16[2,512,512]{2,1,0:T(8,128)(2,1)S(1)}, bf16[2,512,512]{2,1,0:T(8,128)(2,1)}, u32[]{:S(2)}, u32[]{:S(2)}) collective-permute-start(bf16[2,512,512]{2,1,0:T(8,128)(2,1)S(1)} %bitcast.45), channel_id=1, source_target_pairs={{1,0},{2,1},{3,2},{5,4},{6,5},{7,6},{9,8},{10,9},{11,10},{13,12},{... | collective-permute-start | bytes 3145736 | tf_op jit(solution)/shard_map/ppermute | solution.py:227
  16.8 34.4 %collective-permute-done.2 = bf16[2,512,512]{2,1,0:T(8,128)(2,1)} collective-permute-done((bf16[2,512,512]{2,1,0:T(8,128)(2,1)S(1)}, bf16[2,512,512]{2,1,0:T(8,128)(2,1)}, u32[]{:S(2)}, u32[]{:S(2)}) %collective-permute-start.2) | collective-permute-done | bytes 1048608 | tf_op jit(solution)/shard_map/ppermute | solution.py:369
  53.5 7.3 %scan.1 = (bf16[2048,512]{1,0:T(8,128)(2,1)}, bf16[4,256,1024]{2,1,0:T(8,128)(2,1)}) custom-call(bf16[512,2048]{1,0:T(8,128)(2,1)} %get-tuple-element.17.scaled_ref, bf16[512,256]{1,0:T(8,128)(2,1)} %bitcast.49, bf16[512,256]{1,0:T(8,128)(2,1)} %bitcast.51, f32[512,32]{1,0:T(8,128)} %bitcast.40, f32[256,1024]{1,0:T(8,128)} %copy-done.4), custom_call_target="tpu_custom_call" | custom-call | tf_op jit(solution)/shard_map/scan/pallas_call | solution.py:417
  60.8 5.1 %collective-permute-done.4 = bf16[2,512,512]{2,1,0:T(8,128)(2,1)} collective-permute-done((bf16[2,512,512]{2,1,0:T(8,128)(2,1)S(1)}, bf16[2,512,512]{2,1,0:T(8,128)(2,1)}, u32[]{:S(2)}, u32[]{:S(2)}) %collective-permute-start.4) | collective-permute-done | bytes 1048608 | tf_op jit(solution)/shard_map/ppermute | solution.py:227
  65.9 20.6 %collective-permute-done.3 = bf16[2,512,512]{2,1,0:T(8,128)(2,1)} collective-permute-done((bf16[2,512,512]{2,1,0:T(8,128)(2,1)}, bf16[2,512,512]{2,1,0:T(8,128)(2,1)}, u32[]{:S(2)}, u32[]{:S(2)}) %collective-permute-start.3) | collective-permute-done | bytes 1048608 | tf_op jit(solution)/shard_map/ppermute | solution.py:361
  86.5 1.7 select_bitcast_fusion.1
  88.2 1.6 pad_maximum_fusion.mine_ref.slots_ref
  89.8 1.7 dynamic-slice_bitcast_fusion
  93.2 3.8 %collective-permute-done.6.theirs_ref = bf16[4,512,512]{2,1,0:T(8,128)(2,1)} collective-permute-done((bf16[4,512,512]{2,1,0:T(8,128)(2,1)}, bf16[4,512,512]{2,1,0:T(8,128)(2,1)}, u32[]{:S(2)}, u32[]{:S(2)}) %collective-permute-start.6) | collective-permute-done | bytes 2097184 | tf_op jit(solution)/shard_map/ppermute | solution.py:349
  97.0 10.2 %sent.1 = (bf16[2,1024,512]{2,1,0:T(8,128)(2,1)}, bf16[2,1024,512]{2,1,0:T(8,128)(2,1)}) custom-call(s32[9]{0:T(128)} %stack.51.table_ref, bf16[2048,512]{1,0:T(8,128)(2,1)} %get-tuple-element.19.own_ref, bf16[2048,512]{1,0:T(8,128)(2,1)} %copy-done.1, bf16[4,2,512,512]{3,2,1,0:T(8,128)(2,1)} %copy-done, bf16[4,512,512]{2,1,0:T(8,128)(2,1)} %collective-permute-done.6.theirs_ref), custom_call_target="tpu_custom_call" | custom-call | tf_op jit(solution)/shard_map/sent/pallas_call | solution.py:327
  107.8 1.5 collective-permute-start.9
  109.3 15.8 %project.1.grad_ref = bf16[512,2048]{1,0:T(8,128)(2,1)} custom-call(s32[9]{0:T(128)} %stack.51.table_ref, bf16[4,2,512,512]{3,2,1,0:T(8,128)(2,1)} %copy-done, bf16[2048,4096]{1,0:T(8,128)(2,1)} %high_ref.1, bf16[2048,4096]{1,0:T(8,128)(2,1)} %high_ref.1), custom_call_target="tpu_custom_call" | custom-call | tf_op jit(solution)/shard_map/project/pallas_call | solution.py:281
  125.1 6.8 %pulls.1 = (bf16[512,2048]{1,0:T(8,128)(2,1)}, f32[256,1024]{1,0:T(8,128)}) custom-call(bf16[512,2048]{1,0:T(8,128)(2,1)} %project.1.grad_ref, bf16[512,256]{1,0:T(8,128)(2,1)} %bitcast.52, f32[512,32]{1,0:T(8,128)} %bitcast.41), custom_call_target="tpu_custom_call" | custom-call | tf_op jit(solution)/shard_map/pulls/pallas_call | solution.py:421
  133.4 10.3 %kept.1 = (bf16[2,1024,512]{2,1,0:T(8,128)(2,1)}, bf16[2,1024,512]{2,1,0:T(8,128)(2,1)}) custom-call(s32[9]{0:T(128)} %stack.51.table_ref, bf16[2048,512]{1,0:T(8,128)(2,1)} %get-tuple-element.19.own_ref, bf16[2048,512]{1,0:T(8,128)(2,1)} %copy-done.1, bf16[4,2,512,512]{3,2,1,0:T(8,128)(2,1)} %copy-done, bf16[4,512,512]{2,1,0:T(8,128)(2,1)} %collective-permute-done.6.theirs_ref), custom_call_target="tpu_custom_call" | custom-call | tf_op jit(solution)/shard_map/kept/pallas_call | solution.py:327
  143.7 11.5 %collective-permute-done.7 = bf16[2,1024,512]{2,1,0:T(8,128)(2,1)} collective-permute-done((bf16[2,1024,512]{2,1,0:T(8,128)(2,1)}, bf16[2,1024,512]{2,1,0:T(8,128)(2,1)}, u32[]{:S(2)}, u32[]{:S(2)}) %collective-permute-start.7) | collective-permute-done | bytes 2097184 | tf_op jit(solution)/shard_map/ppermute | solution.py:349
  155.2 1.8 fusion.2
  157.0 1.6 collective-permute-start.8
  160.5 9.3 %grads.1 = (bf16[512,2048]{1,0:T(8,128)(2,1)}, bf16[512,256]{1,0:T(8,128)(2,1)}, bf16[512,256]{1,0:T(8,128)(2,1)}) custom-call(bf16[512,2048]{1,0:T(8,128)(2,1)} %get-tuple-element.24.grad_ref, bf16[512,2048]{1,0:T(8,128)(2,1)} %get-tuple-element.17.scaled_ref, bf16[512,256]{1,0:T(8,128)(2,1)} %bitcast.50, bf16[512,256]{1,0:T(8,128)(2,1)} %bitcast.53, ...), custom_call_target="tpu_custom_call" | custom-call | tf_op jit(solution)/shard_map/grads/pallas_call | solution.py:423
  169.8 11.8 %collective-permute-done.8 = bf16[1024,512]{1,0:T(8,128)(2,1)} collective-permute-done((bf16[1024,512]{1,0:T(8,128)(2,1)S(1)}, bf16[1024,512]{1,0:T(8,128)(2,1)}, u32[]{:S(2)}, u32[]{:S(2)}) %collective-permute-start.8) | collective-permute-done | bytes 1048608 | tf_op jit(solution)/shard_map/ppermute | solution.py:349
  181.6 2.3 %fusion.1 = bf16[1024,512]{1,0:T(8,128)(2,1)S(1)} fusion(bf16[1024,512]{1,0:T(8,128)(2,1)} %collective-permute-done.8, bf16[2,1024,512]{2,1,0:T(8,128)(2,1)} %collective-permute-done.7, bf16[2,1024,512]{2,1,0:T(8,128)(2,1)} %get-tuple-element.20), kind=kLoop, calls=%fused_computation.5 | loop fusion | flops 3145728 | bytes 4194304 | tf_op jit(solution)/shard_map/convert_element_type | solution.py:353
  184.3 1.6 fusion
  (31 shorter events, 12.8 us)
Async XLA Ops:
  0.6 2.5 %copy-start.5 = (f32[1,512,32]{1,2,0:T(8,128)S(1)}, f32[1,512,32]{1,2,0:T(8,128)}, u32[]{:S(2)}) copy-start(f32[1,512,32]{1,2,0:T(8,128)} %param.9) | copy-start | bytes 196612
  2.7 48.5 %collective-permute-start.2 = (bf16[2,512,512]{2,1,0:T(8,128)(2,1)S(1)}, bf16[2,512,512]{2,1,0:T(8,128)(2,1)}, u32[]{:S(2)}, u32[]{:S(2)}) collective-permute-start(bf16[2,512,512]{2,1,0:T(8,128)(2,1)S(1)} %bitcast.44), channel_id=1, source_target_pairs={{0,2},{1,3},{2,0},{3,1},{4,6},{5,7},{6,4},{7,5},{8,10},{9,11},{10,... | collective-permute-start | bytes 3145736 | tf_op jit(solution)/shard_map/ppermute | solution.py:369
  10.7 41.8 %collective-permute-start = (f32[256,1024]{1,0:T(8,128)}, f32[256,1024]{1,0:T(8,128)S(1)}, u32[]{:S(2)}, u32[]{:S(2)}) collective-permute-start(f32[256,1024]{1,0:T(8,128)} %get-tuple-element.18), channel_id=1, source_target_pairs={{0,4},{1,5},{2,6},{3,7},{8,12},{9,13},{10,14},{11,15},{16,20},{17,... | collective-permute-start | bytes 3145736 | tf_op jit(solution)/shard_map/ppermute | solution.py:227
  12.2 48.6 %collective-permute-start.5 = (bf16[2,512,512]{2,1,0:T(8,128)(2,1)S(1)}, bf16[2,512,512]{2,1,0:T(8,128)(2,1)}, u32[]{:S(2)}, u32[]{:S(2)}) collective-permute-start(bf16[2,512,512]{2,1,0:T(8,128)(2,1)S(1)} %bitcast.45), channel_id=1, source_target_pairs={{1,0},{2,1},{3,2},{5,4},{6,5},{7,6},{9,8},{10,9},{11,10},{13,12},{... | collective-permute-start | bytes 3145736 | tf_op jit(solution)/shard_map/ppermute | solution.py:227
  15.6 50.4 %collective-permute-start.4 = (bf16[2,512,512]{2,1,0:T(8,128)(2,1)S(1)}, bf16[2,512,512]{2,1,0:T(8,128)(2,1)}, u32[]{:S(2)}, u32[]{:S(2)}) collective-permute-start(bf16[2,512,512]{2,1,0:T(8,128)(2,1)S(1)} %bitcast.46), channel_id=1, source_target_pairs={{0,1},{1,2},{2,3},{4,5},{5,6},{6,7},{8,9},{9,10},{10,11},{12,13},{... | collective-permute-start | bytes 3145736 | tf_op jit(solution)/shard_map/ppermute | solution.py:227
  51.2 35.3 %collective-permute-start.3 = (bf16[2,512,512]{2,1,0:T(8,128)(2,1)}, bf16[2,512,512]{2,1,0:T(8,128)(2,1)}, u32[]{:S(2)}, u32[]{:S(2)}) collective-permute-start(bf16[2,512,512]{2,1,0:T(8,128)(2,1)} %collective-permute-done.2), channel_id=1, source_target_pairs={{1,0},{2,3},{5,4},{6,7},{9,8},{10,11},{13,12},{14,15},{17,16},{18,... | collective-permute-start | bytes 3145736 | tf_op jit(solution)/shard_map/ppermute | solution.py:361
  52.5 1.0 copy-start.4
  60.8 32.4 %collective-permute-start.1 = (bf16[2048,512]{1,0:T(8,128)(2,1)}, bf16[2048,512]{1,0:T(8,128)(2,1)S(1)}, u32[]{:S(2)}, u32[]{:S(2)}) collective-permute-start(bf16[2048,512]{1,0:T(8,128)(2,1)} %get-tuple-element.19.own_ref), channel_id=1, source_target_pairs={{0,4},{4,0},{1,5},{5,1},{2,6},{6,2},{3,7},{7,3},{8,12},{12,8},{9,1... | collective-permute-start | bytes 6291464 | tf_op jit(solution)/shard_map/ppermute | solution.py:349
  89.8 2.7 %copy-start = (bf16[4,2,512,512]{3,2,1,0:T(8,128)(2,1)}, bf16[4,2,512,512]{3,2,1,0:T(8,128)(2,1)S(1)}, u32[]{:S(2)}) copy-start(bf16[4,2,512,512]{3,2,1,0:T(8,128)(2,1)S(1)} %pad_maximum_fusion.mine_ref.slots_ref) | copy-start | bytes 12582916
  92.5 4.5 %collective-permute-start.6 = (bf16[4,512,512]{2,1,0:T(8,128)(2,1)}, bf16[4,512,512]{2,1,0:T(8,128)(2,1)}, u32[]{:S(2)}, u32[]{:S(2)}) collective-permute-start(bf16[4,512,512]{2,1,0:T(8,128)(2,1)} %dynamic-slice_bitcast_fusion), channel_id=1, source_target_pairs={{0,4},{4,0},{1,5},{5,1},{2,6},{6,2},{3,7},{7,3},{8,12},{12,8},{9,1... | collective-permute-start | bytes 6291464 | tf_op jit(solution)/shard_map/ppermute | solution.py:349
  93.2 3.8 %copy-start.1 = (bf16[2048,512]{1,0:T(8,128)(2,1)}, bf16[2048,512]{1,0:T(8,128)(2,1)S(1)}, u32[]{:S(2)}) copy-start(bf16[2048,512]{1,0:T(8,128)(2,1)S(1)} %collective-permute-done.1.other_ref) | copy-start | bytes 6291460
  107.2 48.0 %collective-permute-start.7 = (bf16[2,1024,512]{2,1,0:T(8,128)(2,1)}, bf16[2,1024,512]{2,1,0:T(8,128)(2,1)}, u32[]{:S(2)}, u32[]{:S(2)}) collective-permute-start(bf16[2,1024,512]{2,1,0:T(8,128)(2,1)} %get-tuple-element.21), channel_id=1, source_target_pairs={{0,8},{8,0},{16,24},{24,16},{1,9},{9,1},{17,25},{25,17},{2,10},{10... | collective-permute-start | bytes 6291464 | tf_op jit(solution)/shard_map/ppermute | solution.py:349
  107.8 50.9 %collective-permute-start.9 = (bf16[2,1024,512]{2,1,0:T(8,128)(2,1)}, bf16[2,1024,512]{2,1,0:T(8,128)(2,1)S(1)}, u32[]{:S(2)}, u32[]{:S(2)}) collective-permute-start(bf16[2,1024,512]{2,1,0:T(8,128)(2,1)} %get-tuple-element.23), channel_id=1, source_target_pairs={{0,16},{8,24},{16,0},{24,8},{1,17},{9,25},{17,1},{25,9},{2,18},{10... | collective-permute-start | bytes 6291464 | tf_op jit(solution)/shard_map/ppermute | solution.py:349
  131.9 28.5 %collective-permute-start.11 = (f32[256,1024]{1,0:T(8,128)}, f32[256,1024]{1,0:T(8,128)}, u32[]{:S(2)}, u32[]{:S(2)}) collective-permute-start(f32[256,1024]{1,0:T(8,128)} %get-tuple-element.26), channel_id=1, source_target_pairs={{4,0},{5,1},{6,2},{7,3},{12,8},{13,9},{14,10},{15,11},{20,16},{21,... | collective-permute-start | bytes 3145736 | tf_op jit(solution)/shard_map/ppermute | solution.py:227
  143.7 15.0 %copy-start.2 = (bf16[2,1024,512]{2,1,0:T(8,128)(2,1)S(1)}, bf16[2,1024,512]{2,1,0:T(8,128)(2,1)}, u32[]{:S(2)}) copy-start(bf16[2,1024,512]{2,1,0:T(8,128)(2,1)} %get-tuple-element.22) | copy-start | bytes 6291460
  157.0 24.5 %collective-permute-start.8 = (bf16[1024,512]{1,0:T(8,128)(2,1)S(1)}, bf16[1024,512]{1,0:T(8,128)(2,1)}, u32[]{:S(2)}, u32[]{:S(2)}) collective-permute-start(bf16[1024,512]{1,0:T(8,128)(2,1)S(1)} %fusion.2), channel_id=1, source_target_pairs={{0,16},{8,24},{16,0},{24,8},{1,17},{9,25},{17,1},{25,9},{2,18},{10... | collective-permute-start | bytes 3145736 | tf_op jit(solution)/shard_map/ppermute | solution.py:349
  159.9 24.4 %collective-permute-start.10 = (bf16[1024,512]{1,0:T(8,128)(2,1)}, bf16[1024,512]{1,0:T(8,128)(2,1)}, u32[]{:S(2)}, u32[]{:S(2)}) collective-permute-start(bf16[1024,512]{1,0:T(8,128)(2,1)} %fusion.3), channel_id=1, source_target_pairs={{0,8},{8,0},{16,24},{24,16},{1,9},{9,1},{17,25},{25,17},{2,10},{10... | collective-permute-start | bytes 3145736 | tf_op jit(solution)/shard_map/ppermute | solution.py:349
  169.8 14.5 %copy-start.3 = (bf16[2,1024,512]{2,1,0:T(8,128)(2,1)S(1)}, bf16[2,1024,512]{2,1,0:T(8,128)(2,1)}, u32[]{:S(2)}) copy-start(bf16[2,1024,512]{2,1,0:T(8,128)(2,1)} %get-tuple-element.22) | copy-start | bytes 6291460
where the time goes:
time: 188 us; the launch traced here: 187 us
  waiting for transfers between devices  87.7 us (47%)
  Pallas kernels  66.5 us (35%)
  starting transfers between devices  13.5 us (7%)
  other arithmetic  11.8 us (6%)
  local copies, waits for them, and re-layouts  7.24 us (4%)
    ppermute x1, waiting for transfers between devices, swapped_across(): return lax.ppermute(own, 'tensor', [(i, (i + 2) % 4) for i in range(4)])  34.4 us
    ppermute x6, waiting for transfers between devices, swapped(): lax.ppermute(value, axis, [(i, i ^ by) for i in range(lax.axis_size(axis))])  27.6 us
    ppermute x1, waiting for transfers between devices, gathered(): far = lax.ppermute(across, 'tensor', [(1, 0), (2, 3)])  20.6 us
    pallas_call x2, Pallas kernels, partials(): pl.pallas_call(partial_kernel, grid_spec=pltpu.PrefetchScalarGridSpec(num...  20.5 us
    pallas_call x1, Pallas kernels, project(): pl.pallas_call(functools.partial(project_kernel, first=first, last=last),...  15.8 us
    pallas_call x1, Pallas kernels, per_device(): grads(grad, scaled, b_in, c_in, log_decay, held, leaving)  9.32 us
    ppermute x4, starting transfers between devices, passed_along(): return lax.ppermute(shard, axis, pairs)  7.59 us
    pallas_call x1, Pallas kernels, per_device(): rows_t, held = scan(scaled, b_in, c_in, log_decay, entering)  7.3 us
  transfers between devices with their start and end apart: 12, of which 7 were waited for; matrix products, arithmetic and copies ran while one was open for 6% of the time, Pallas kernels for 30%

commit v1 on v0

--- a/solution.py
+++ b/solution.py
@@ -7,11 +7,13 @@
 from jax.experimental.pallas import tpu as pltpu
 from jax.sharding import PartitionSpec as P
 
+
 HEAD_DIM = 64
 STATE = 128
 CHUNK = 128
 LANES = 128
-PARTS = 1
+PARTS = 2
+THIS_MESH = (4, 2, 4)
 
 BF16 = jnp.bfloat16
 F32 = jnp.float32
@@ -38,7 +40,7 @@
     rest = decays - first.astype(F32)
     second = rest.astype(BF16)
     third = (rest - second.astype(F32)).astype(BF16)
-    running = dot(ones, first, NN) + dot(ones, second, NN) + dot(ones, third, NN)
+    running = dot(ones, first, NT) + dot(ones, second, NT) + dot(ones, third, NT)
     half = 0.5 * running[CHUNK - 1 : CHUNK, :]
     return jnp.exp(running - half), jnp.exp(half - running), jnp.exp(half)
 
@@ -176,6 +178,8 @@
     def back(cols):
         return pl.BlockSpec((CHUNK, cols), lambda i: (chunks - 1 - i, 0))
 
+    decays_ahead = pl.BlockSpec((heads, CHUNK), lambda i: (0, i))
+    decays_back = pl.BlockSpec((heads, CHUNK), lambda i: (0, chunks - 1 - i))
     whole = pl.BlockSpec((keys, width), lambda i: (0, 0))
     state_type = jax.ShapeDtypeStruct((keys, width), F32)
     rows_type = jax.ShapeDtypeStruct((tokens, inner), BF16)
@@ -184,14 +188,14 @@
     scratch = [pltpu.VMEM((keys, width), F32)]
     states = call(
         functools.partial(states_kernel, groups=groups),
-        in_specs=[ahead(inner), ahead(keys), ahead(heads)],
+        in_specs=[ahead(inner), ahead(keys), decays_ahead],
         out_specs=[ahead(inner), whole],
         out_shape=[rows_type, state_type],
         name="states",
     )
     scan = call(
         functools.partial(scan_kernel, groups=groups),
-        in_specs=[ahead(inner), ahead(keys), ahead(keys), ahead(heads), whole],
+        in_specs=[ahead(inner), ahead(keys), ahead(keys), decays_ahead, whole],
         out_specs=[
             pl.BlockSpec((inner, CHUNK), lambda i: (0, i)),
             pl.BlockSpec((1, keys, width), lambda i: (i, 0, 0)),
@@ -202,7 +206,7 @@
     )
     pulls = call(
         functools.partial(pulls_kernel, groups=groups),
-        in_specs=[back(inner), back(keys), back(heads)],
+        in_specs=[back(inner), back(keys), decays_back],
         out_specs=[back(inner), whole],
         out_shape=[rows_type, state_type],
         name="pulls",
@@ -210,7 +214,7 @@
     grads = call(
         functools.partial(grads_kernel, groups=groups),
         in_specs=[
-            back(inner), back(inner), back(keys), back(keys), back(heads),
+            back(inner), back(inner), back(keys), back(keys), decays_back,
             pl.BlockSpec((1, keys, width), lambda i: (chunks - 1 - i, 0, 0)), whole,
         ],
         out_specs=[back(inner), back(keys), back(keys)],
@@ -231,7 +235,7 @@
     incoming = passed_along(local, axis, by)
     turns = lax.axis_size(axis) - 1
     if turns > 1:
-        total = jnp.exp(jnp.sum(log_decay, axis=0)).reshape(groups, 1, -1)
+        total = jnp.exp(jnp.sum(log_decay, axis=1)).reshape(groups, 1, -1)
         spread = jnp.repeat(total, HEAD_DIM, axis=2)
         spread = jnp.broadcast_to(spread, (groups, STATE, spread.shape[2]))
         spread = spread.reshape(local.shape)
@@ -255,38 +259,51 @@
     return y_grad, weight_grad
 
 
-def project_kernel(table_ref, slots_ref, low_ref, high_ref, *refs, first, last):
+def project_kernel(
+    table_ref, zero_ref, one_ref, two_ref, mid_ref, end_ref, rest_ref, near_ref, far_ref, *refs,
+    first,
+):
     step = pl.program_id(0)
     out_ref, total_ref = refs[-2:]
-    got = dot(slots_ref[0, 0], low_ref[...], NT) + dot(slots_ref[0, 1], high_ref[...], NT)
+
+    def add(own):
+        got = dot(own, near_ref[...], NT) + dot(rest_ref[0], far_ref[...], NT)
+        return got
 
     @pl.when(step == 0)
     def _():
+        got = add(zero_ref[0])
         total_ref[...] = got if first else refs[0][...] + got
 
-    @pl.when(step > 0)
-    def _():
-        total_ref[...] += got
-
-    @pl.when(step == pl.num_programs(0) - 1)
-    def _():
-        out_ref[...] = total_ref[...].astype(out_ref.dtype)
-
-
-def project(table, slots, out_weight, part, parts, before):
-    tokens, wide = slots.shape[2:]
+    @pl.when(step == 1)
+    def _():
+        total_ref[...] += add(one_ref[0])
+
+    @pl.when(step == 2)
+    def _():
+        total_ref[...] += add(two_ref[0])
+
+    @pl.when(step == 3)
+    def _():
+        out_ref[...] = (total_ref[...] + add(mid_ref[0] + end_ref[0])).astype(out_ref.dtype)
+
+
+def project(table, slots, rest, out_weight, part, parts, before):
+    tokens, wide = rest.shape[1:]
     inner = out_weight.shape[0]
     first, last = before is None, part == parts - 1
     whole = pl.BlockSpec((tokens, inner), lambda i, t: (0, 0))
+    held = pl.BlockSpec((1, tokens, wide), lambda i, t: (0, 0, 0))
     return pl.pallas_call(
-        functools.partial(project_kernel, first=first, last=last),
+        functools.partial(project_kernel, first=first),
         grid_spec=pltpu.PrefetchScalarGridSpec(
             num_scalar_prefetch=1,
             grid=(4,),
-            in_specs=[
-                pl.BlockSpec((1, 2, tokens, wide), lambda i, t: (i, 0, 0, 0)),
-                pl.BlockSpec((inner, wide), lambda i, t: (0, t[4 + i] * 2 * parts + part)),
-                pl.BlockSpec((inner, wide), lambda i, t: (0, (t[4 + i] * 2 + 1) * parts + part)),
+            in_specs=[held] * 5
+            + [
+                pl.BlockSpec((1, tokens, wide), lambda i, t: (i, 0, 0)),
+                pl.BlockSpec((inner, wide), lambda i, t: (0, t[4 + i] * parts + part)),
+                pl.BlockSpec((inner, wide), lambda i, t: (0, t[8 + i] * parts + part)),
             ]
             + ([] if first else [whole]),
             out_specs=whole,
@@ -294,55 +311,82 @@
         ),
         out_shape=jax.ShapeDtypeStruct((tokens, inner), BF16 if last else F32),
         name="project",
-    )(table, slots, out_weight, out_weight, *([] if first else [before]))
-
-
-def partial_kernel(table_ref, own_ref, other_ref, mine_ref, theirs_ref, x_ref, y_ref):
+    )(table, *slots, rest, out_weight, out_weight, *([] if first else [before]))
+
+
+def partial_kernel(
+    table_ref, own_ref, other_ref, zero_ref, one_ref, two_ref, mid_ref, end_ref, *refs, targets,
+):
     step = pl.program_id(0)
-    got = dot(own_ref[...], mine_ref[0, 0], NN) + dot(other_ref[...], theirs_ref[0], NN)
-    got = got.astype(BF16)
-
-    @pl.when(step < 2)
-    def _():
-        x_ref[0] = got
-
-    @pl.when(step >= 2)
-    def _():
-        y_ref[0] = got
-
-
-def partials(table, own, other, slots, theirs, targets, name):
+    half_steps = pl.num_programs(0) // 2
+    x_ref, y_ref = refs[:2]
+    picked_ref = refs[-1]
+    wide = zero_ref.shape[2]
+
+    @pl.when(step == 0)
+    def _():
+        last = mid_ref[...] + end_ref[...]
+        if len(refs) == 4:
+            for q, ref in enumerate((zero_ref, one_ref, two_ref)):
+                refs[2][q] = ref[1]
+            refs[2][3] = last[1]
+        for place, target in enumerate(targets):
+            cols = slice(place % 2 * wide, (place % 2 + 1) * wide)
+            slot = table_ref[target]
+            for q, ref in enumerate((zero_ref, one_ref, two_ref)):
+
+                @pl.when(slot == q)
+                def _():
+                    picked_ref[place // 2, :, :, cols] = ref[...]
+
+            @pl.when(slot == 3)
+            def _():
+                picked_ref[place // 2, :, :, cols] = last
+
+    def put(side, ref):
+        got = dot(own_ref[...], picked_ref[side, 0], NN)
+        got += dot(other_ref[...], picked_ref[side, 1], NN)
+        got = got.astype(BF16)
+        ref[0] = got[:, :wide]
+        ref[1] = got[:, wide:]
+
+    @pl.when(step < half_steps)
+    def _():
+        put(0, x_ref)
+
+    @pl.when(step >= half_steps)
+    def _():
+        put(1, y_ref)
+
+
+def partials(table, own, other, slots, targets, with_rest):
     inner, tokens = own.shape
-    half = inner // 2
-    wide = slots.shape[3]
-
-    def slot(i, t):
-        picked = t[targets[3]]
-        for place in (2, 1, 0):
-            picked = jnp.where(i == place, t[targets[place]], picked)
-        return picked
-
-    rows = pl.BlockSpec((half, tokens), lambda i, t: (i // 2, 0))
-    out_type = jax.ShapeDtypeStruct((2, half, wide), BF16)
+    wide = slots[0].shape[2]
+    steps = 4
+    tall = inner // steps
+    half_steps = steps // 2
+    rows = pl.BlockSpec((tall, tokens), lambda i, t: (i, 0))
+    held = pl.BlockSpec((2, tokens, wide), lambda i, t: (0, 0, 0))
+    out_type = jax.ShapeDtypeStruct((2, inner // 2, wide), BF16)
+    out_specs = [
+        pl.BlockSpec((2, tall, wide), lambda i, t: (0, jnp.minimum(i, half_steps - 1), 0)),
+        pl.BlockSpec((2, tall, wide), lambda i, t: (0, jnp.maximum(i - half_steps, 0), 0)),
+    ]
+    out_shape = [out_type, out_type]
+    if with_rest:
+        out_specs.append(pl.BlockSpec((4, tokens, wide), lambda i, t: (0, 0, 0)))
+        out_shape.append(jax.ShapeDtypeStruct((4, tokens, wide), BF16))
     return pl.pallas_call(
-        partial_kernel,
+        functools.partial(partial_kernel, targets=targets),
         grid_spec=pltpu.PrefetchScalarGridSpec(
             num_scalar_prefetch=1,
-            grid=(4,),
-            in_specs=[
-                rows,
-                rows,
-                pl.BlockSpec((1, 1, tokens, wide), lambda i, t: (slot(i, t), t[8], 0, 0)),
-                pl.BlockSpec((1, tokens, wide), lambda i, t: (slot(i, t), 0, 0)),
-            ],
-            out_specs=[
-                pl.BlockSpec((1, half, wide), lambda i, t: (jnp.minimum(i, 1), 0, 0)),
-                pl.BlockSpec((1, half, wide), lambda i, t: (jnp.maximum(i - 2, 0), 0, 0)),
-            ],
+            grid=(steps,),
+            in_specs=[rows, rows] + [held] * 5,
+            out_specs=out_specs,
+            scratch_shapes=[pltpu.VMEM((2, 2, tokens, 2 * wide), BF16)],
         ),
-        out_shape=[out_type, out_type],
-        name=name,
-    )(table, own, other, slots, theirs)
+        out_shape=out_shape,
+    )(table, own, other, *slots)
 
 
 def swapped(value, axis, by):
@@ -353,47 +397,59 @@
     return functools.reduce(jnp.add, [t.astype(F32) for t in terms]).astype(BF16)
 
 
-def gathered(own, place, after):
-    own = own if after is None else lax.optimization_barrier((own, after))[0]
-    up = passed_along(own, "tensor", 1)
-    down = passed_along(own, "tensor", -1)
-    across = swapped_across(own)
-    far = lax.ppermute(across, "tensor", [(1, 0), (2, 3)])
-    slots = jnp.stack(
-        [own, jnp.where(place == 0, far, up), across, jnp.where(place == 3, far, down)]
-    )
-    return slots, across
-
-
-def swapped_across(own):
-    return lax.ppermute(own, "tensor", [(i, (i + 2) % 4) for i in range(4)])
-
-
-def this_mesh(rows_t, out_grad, out_weight):
-    tokens, features = out_grad.shape
+def after(value, *others):
+    return lax.optimization_barrier((value, *others))[0]
+
+
+def gathered(own, held_up):
+    two = swapped(own, "tensor", 2)
+    one = swapped(own, "tensor", 1)
+    own_late, two_late = own, two
+    if held_up:
+        own_late, two_late = lax.optimization_barrier((own, two, *held_up))[:2]
+    end = lax.ppermute(two_late, "tensor", [(1, 0), (2, 3)])
+    mid = lax.ppermute(own_late, "tensor", [(1, 2), (2, 1)])
+    return own, one, two, mid, end
+
+
+def core_halves(out_grad):
+    half = out_grad.shape[1] // 2
+    core = lax.axis_index("seq")
+    mine = lax.dynamic_slice_in_dim(out_grad, core * half, half, 1)
+    theirs = lax.dynamic_slice_in_dim(out_grad, (1 - core) * half, half, 1)
+    return jnp.stack([mine, swapped(theirs, "seq", 1)])
+
+
+def this_mesh(rows_t, both, out_weight):
     parts = PARTS
-    wide = features // 2 // parts
+    wide = both.shape[2] // parts
     place = lax.axis_index("tensor")
     repo = lax.axis_index("dp")
     core = lax.axis_index("seq")
     table = jnp.stack(
-        [(place - (repo ^ r)) % 4 for r in range(4)]
-        + [(place - s) % 4 for s in range(4)]
-        + [core]
+        [place ^ repo ^ r for r in range(4)]
+        + [(place ^ q) * 2 + core for q in range(4)]
+        + [(place ^ q) * 2 + 1 - core for q in range(4)]
     ).astype(jnp.int32)
-    split = out_grad.reshape(tokens, 2, parts, wide).transpose(2, 1, 0, 3)
     other = swapped(rows_t, "seq", 1)
     y_grad = None
-    after = None
     pieces = []
+    ahead = late = None
     for part in range(parts):
-        slots, after = gathered(split[part], place, after)
-        theirs = lax.dynamic_index_in_dim(slots, 1 - core, 1, keepdims=False)
-        theirs = swapped(theirs, "seq", 1)
-        x_send, y_send = partials(table, rows_t, other, slots, theirs, (1, 3, 2, 3), "sent")
+        own = lax.slice_in_dim(both, part * wide, (part + 1) * wide, axis=2)
+        if ahead is not None:
+            own = after(own, *ahead)
+        own, one, two, mid, end = gathered(own, late)
+        ahead = (mid, end)
+        if part > 0:
+            end = after(end, y_grad, x_kept, y_kept)
+        slots = own, one, two, mid, end
+        x_send, y_send, rest = partials(table, rows_t, other, slots, (1, 3, 2, 3), True)
+        late = (x_send,)
         x_got = swapped(x_send, "dp", 1)
         y_got = swapped(y_send, "dp", 2)
-        x_kept, y_kept = partials(table, rows_t, other, slots, theirs, (0, 2, 0, 1), "kept")
+        rest = swapped(rest, "seq", 1)
+        x_kept, y_kept = partials(table, rows_t, other, slots, (0, 2, 0, 1), False)
         x_last = swapped(total(x_kept[1], x_got[1]), "dp", 2)
         y_last = swapped(total(y_kept[1], y_got[1]), "dp", 1)
         pieces.append(
@@ -401,7 +457,7 @@
                 [total(x_kept[0], x_got[0], x_last), total(y_kept[0], y_got[0], y_last)]
             )
         )
-        y_grad = project(table, slots, out_weight, part, parts, y_grad)
+        y_grad = project(table, slots, rest, out_weight, part, parts, y_grad)
     return y_grad, jnp.concatenate(pieces, axis=1)
 
 
@@ -410,14 +466,21 @@
         x_in[0], b_in[0], c_in[0], log_decay[0], out_grad[0],
     )
     tokens, heads = log_decay.shape
+    log_decay = log_decay.T
     groups = b_in.shape[1] // STATE
+    sizes = tuple(lax.axis_size(name) for name in ("dp", "seq", "tensor"))
+    here = sizes == THIS_MESH
+    if here:
+        both = core_halves(out_grad)
+        log_decay, both = lax.optimization_barrier((log_decay, both))
     states, scan, pulls, grads = scan_calls(tokens, heads, groups)
     scaled, end_local = states(x_in, b_in, log_decay)
     entering = chained(end_local, log_decay, groups, "seq", 1)
     rows_t, held = scan(scaled, b_in, c_in, log_decay, entering)
-    sizes = tuple(lax.axis_size(name) for name in ("dp", "seq", "tensor"))
-    project_both = this_mesh if sizes == (4, 2, 4) else any_mesh
-    y_grad, weight_grad = project_both(rows_t, out_grad, out_weight)
+    if here:
+        y_grad, weight_grad = this_mesh(rows_t, both, out_weight)
+    else:
+        y_grad, weight_grad = any_mesh(rows_t, out_grad, out_weight)
     grad, start_local = pulls(y_grad, c_in, log_decay)
     leaving = chained(start_local, log_decay, groups, "seq", -1)
     x_grad, b_grad, c_grad = grads(grad, scaled, b_in, c_in, log_decay, held, leaving)
@@ -426,6 +489,7 @@
 
 def solution(mesh):
     tokens_spec = P("dp", "seq", "tensor")
+
     return jax.shard_map(
         per_device,
         mesh=mesh,

time: 188 us -> 223 us (1.19); the launches traced: 187 us -> 219 us
  Pallas kernels: 66.5 us -> 83.3 us
  starting transfers between devices: 13.5 us -> 24.4 us
    ppermute x6 -> x16, waiting for transfers between devices: 27.6 us -> 71.4 us  [swapped(): lax.ppermute(value, axis, [(i, i ^ by) for i in range(lax.axis_size(axis))])]
    ppermute x2 -> x4, waiting for transfers between devices: 54.9 us -> 13.8 us  [the longest x2 13.8 us: gathered(): end = lax.ppermute(two_late, 'tensor', [(1, 0), (2, 3)])]
    pallas_call x3 -> x6, Pallas kernels: 36.3 us -> 53.3 us  [the longest x4 31 us: partials(): pl.pallas_call(functools.partial(partial_kernel, targets=targets), grid_s...]
    ppermute x6 -> x16, starting transfers between devices: 4.18 us -> 15.9 us  [swapped(): lax.ppermute(value, axis, [(i, i ^ by) for i in range(lax.axis_size(axis))])]
    convert_element_type x4 -> x8, other arithmetic: 7.04 us -> 11.2 us  [total(): functools.reduce(jnp.add, [t.astype(F32) for t in terms]).astype(BF16)]
    ppermute x4 -> x2, starting transfers between devices: 7.59 us -> 3.65 us  [passed_along(): return lax.ppermute(shard, axis, pairs)]
    ppermute x2 -> x4, starting transfers between devices: 1.68 us -> 4.91 us  [the longest x2 2.56 us: gathered(): end = lax.ppermute(two_late, 'tensor', [(1, 0), (2, 3)])]
    ppermute x4 -> x2, waiting for transfers between devices: 5.15 us -> 2.42 us  [passed_along(): return lax.ppermute(shard, axis, pairs)]
  transfers between devices with their start and end apart: 12 -> 22, of which waited for: 7 -> 8; matrix products, arithmetic and copies ran while one was open for 6% -> 7% of each run, Pallas kernels for 30% -> 24%
where the time goes in v1:
time: 223 us; the launch traced here: 219 us
  waiting for transfers between devices  87.6 us (39%)
  Pallas kernels  83.3 us (37%)
  starting transfers between devices  24.4 us (11%)
  other arithmetic  13.8 us (6%)
  local copies, waits for them, and re-layouts  9.06 us (4%)
    ppermute x16, waiting for transfers between devices, swapped(): lax.ppermute(value, axis, [(i, i ^ by) for i in range(lax.axis_size(axis))])  71.4 us
    pallas_call x4, Pallas kernels, partials(): pl.pallas_call(functools.partial(partial_kernel, targets=targets), grid_s...  31 us
    pallas_call x2, Pallas kernels, project(): pl.pallas_call(functools.partial(project_kernel, first=first), grid_spec=...  22.3 us
    ppermute x16, starting transfers between devices, swapped(): lax.ppermute(value, axis, [(i, i ^ by) for i in range(lax.axis_size(axis))])  15.9 us
    ppermute x2, waiting for transfers between devices, gathered(): end = lax.ppermute(two_late, 'tensor', [(1, 0), (2, 3)])  13.8 us
    convert_element_type x8, other arithmetic, total(): functools.reduce(jnp.add, [t.astype(F32) for t in terms]).astype(BF16)  11.2 us
    pallas_call x1, Pallas kernels, per_device(): grads(grad, scaled, b_in, c_in, log_decay, held, leaving)  9.29 us
    pallas_call x1, Pallas kernels, per_device(): rows_t, held = scan(scaled, b_in, c_in, log_decay, entering)  7.27 us
  transfers between devices with their start and end apart: 22, of which 8 were waited for; matrix products, arithmetic and copies ran while one was open for 7% of the time, Pallas kernels for 24%

profile of v1, /device:TPU:26, one launch (start us, length us, event | category | flops | bytes accessed | tf_op | source)
XLA Modules:
  0.0 219.3 jit_solution(11249699010231782757)
XLA Ops:
  2.0 1.9 collective-permute-done
  5.0 6.6 %states.1 = (bf16[512,2048]{1,0:T(8,128)(2,1)}, f32[256,1024]{1,0:T(8,128)}) custom-call(bf16[512,2048]{1,0:T(8,128)(2,1)} %bitcast.54, bf16[512,256]{1,0:T(8,128)(2,1)} %bitcast.48, f32[32,512]{1,0:T(8,128)} %bitcast.55), custom_call_target="tpu_custom_call" | custom-call | tf_op jit(solution)/shard_map/states/pallas_call | solution.py:477
  11.6 2.1 collective-permute-start.1
  13.7 2.4 %collective-permute-done.1.enter_ref = f32[256,1024]{1,0:T(8,128)S(1)} collective-permute-done((f32[256,1024]{1,0:T(8,128)}, f32[256,1024]{1,0:T(8,128)S(1)}, u32[]{:S(2)}, u32[]{:S(2)}) %collective-permute-start.1) | collective-permute-done | bytes 1048608 | tf_op jit(solution)/shard_map/ppermute | solution.py:231
  17.1 7.3 %scan.1 = (bf16[2048,512]{1,0:T(8,128)(2,1)}, bf16[4,256,1024]{2,1,0:T(8,128)(2,1)}) custom-call(bf16[512,2048]{1,0:T(8,128)(2,1)} %get-tuple-element.30.scaled_ref, bf16[512,256]{1,0:T(8,128)(2,1)} %bitcast.49, bf16[512,256]{1,0:T(8,128)(2,1)} %bitcast.51, f32[32,512]{1,0:T(8,128)} %bitcast.56, f32[256,1024]{1,0:T(8,128)} %copy-done.9), custom_call_target="tpu_custom_call" | custom-call | tf_op jit(solution)/shard_map/scan/pallas_call | solution.py:479
  27.9 3.6 %collective-permute-start.3 = (bf16[2,512,256]{2,1,0:T(8,128)(2,1)S(1)}, bf16[2,512,256]{2,1,0:T(8,128)(2,1)}, u32[]{:S(2)}, u32[]{:S(2)}) collective-permute-start(bf16[2,512,256]{2,1,0:T(8,128)(2,1)S(1)} %get-tuple-element.54.zero_ref), channel_id=1, source_target_pairs={{0,1},{1,0},{2,3},{3,2},{4,5},{5,4},{6,7},{7,6},{8,9},{9,8},{10,11... | collective-permute-start | bytes 1572872 | tf_op jit(solution)/shard_map/ppermute | solution.py:393
  31.6 20.8 %collective-permute-done.4.two_ref = bf16[2,512,256]{2,1,0:T(8,128)(2,1)} collective-permute-done((bf16[2,512,256]{2,1,0:T(8,128)(2,1)S(1)}, bf16[2,512,256]{2,1,0:T(8,128)(2,1)}, u32[]{:S(2)}, u32[]{:S(2)}) %collective-permute-start.4) | collective-permute-done | bytes 524320 | tf_op jit(solution)/shard_map/ppermute | solution.py:393
  54.5 13.8 %collective-permute-done.6.end_ref = bf16[2,512,256]{2,1,0:T(8,128)(2,1)} collective-permute-done((bf16[2,512,256]{2,1,0:T(8,128)(2,1)}, bf16[2,512,256]{2,1,0:T(8,128)(2,1)}, u32[]{:S(2)}, u32[]{:S(2)}) %collective-permute-start.6) | collective-permute-done | bytes 524320 | tf_op jit(solution)/shard_map/ppermute | solution.py:410
  69.6 7.9 %shard_map.94 = (bf16[2,1024,256]{2,1,0:T(8,128)(2,1)}, bf16[2,1024,256]{2,1,0:T(8,128)(2,1)}, bf16[4,512,256]{2,1,0:T(8,128)(2,1)}) custom-call(s32[12]{0:T(128)} %stack.58.table_ref, bf16[2048,512]{1,0:T(8,128)(2,1)} %get-tuple-element.32.own_ref, bf16[2048,512]{1,0:T(8,128)(2,1)} %copy-done, bf16[2,512,256]{2,1,0:T(8,128)(2,1)} %copy-done.2, ...), custom_call_target="tpu_custom_call" | custom-call | tf_op jit(solution)/shard_map/pallas_call | solution.py:379
  77.7 1.6 collective-permute-start.9
  79.3 23.8 %collective-permute-done.12.two_ref = bf16[2,512,256]{2,1,0:T(8,128)(2,1)S(1)} collective-permute-done((bf16[2,512,256]{2,1,0:T(8,128)(2,1)S(1)}, bf16[2,512,256]{2,1,0:T(8,128)(2,1)S(1)}, u32[]{:S(2)}, u32[]{:S(2)}) %collective-permute-start.12) | collective-permute-done | bytes 524320 | tf_op jit(solution)/shard_map/ppermute | solution.py:393
  104.4 2.7 %collective-permute-start.11 = (bf16[2,512,256]{2,1,0:T(8,128)(2,1)S(1)}, bf16[2,512,256]{2,1,0:T(8,128)(2,1)S(1)}, u32[]{:S(2)}, u32[]{:S(2)}) collective-permute-start(bf16[2,512,256]{2,1,0:T(8,128)(2,1)S(1)} %get-tuple-element.39.zero_ref), channel_id=1, source_target_pairs={{0,1},{1,0},{2,3},{3,2},{4,5},{5,4},{6,7},{7,6},{8,9},{9,8},{10,11... | collective-permute-start | bytes 1572872 | tf_op jit(solution)/shard_map/ppermute | solution.py:393
  108.6 7.6 %shard_map.93 = (bf16[2,1024,256]{2,1,0:T(8,128)(2,1)}, bf16[2,1024,256]{2,1,0:T(8,128)(2,1)}) custom-call(s32[12]{0:T(128)} %stack.58.table_ref, bf16[2048,512]{1,0:T(8,128)(2,1)} %get-tuple-element.32.own_ref, bf16[2048,512]{1,0:T(8,128)(2,1)} %copy-done, bf16[2,512,256]{2,1,0:T(8,128)(2,1)} %copy-done.2, ...), custom_call_target="tpu_custom_call" | custom-call | tf_op jit(solution)/shard_map/pallas_call | solution.py:379
  116.2 10.7 %project.2.refs_0_ = f32[512,2048]{1,0:T(8,128)} custom-call(s32[12]{0:T(128)} %stack.58.table_ref, bf16[2,512,256]{2,1,0:T(8,128)(2,1)} %copy-done.2, bf16[2,512,256]{2,1,0:T(8,128)(2,1)} %collective-permute-done.3.one_ref, bf16[2,512,256]{2,1,0:T(8,128)(2,1)} %collective-permute-done.4.two_ref, bf16[2,512,256]{2,1,0:T(8,128)(2,1)} %collective-permute-done.5.mid_ref, ...), custom_call_target="tpu_custom_call" | custom-call | tf_op jit(solution)/shard_map/project/pallas_call | solution.py:297
  126.9 3.2 %collective-permute-done.11.one_ref = bf16[2,512,256]{2,1,0:T(8,128)(2,1)S(1)} collective-permute-done((bf16[2,512,256]{2,1,0:T(8,128)(2,1)S(1)}, bf16[2,512,256]{2,1,0:T(8,128)(2,1)S(1)}, u32[]{:S(2)}, u32[]{:S(2)}) %collective-permute-start.11) | collective-permute-done | bytes 524320 | tf_op jit(solution)/shard_map/ppermute | solution.py:393
  131.7 7.9 %shard_map.96 = (bf16[2,1024,256]{2,1,0:T(8,128)(2,1)}, bf16[2,1024,256]{2,1,0:T(8,128)(2,1)}, bf16[4,512,256]{2,1,0:T(8,128)(2,1)}) custom-call(s32[12]{0:T(128)} %stack.58.table_ref, bf16[2048,512]{1,0:T(8,128)(2,1)} %get-tuple-element.32.own_ref, bf16[2048,512]{1,0:T(8,128)(2,1)} %copy-done, bf16[2,512,256]{2,1,0:T(8,128)(2,1)} %copy-done.1, ...), custom_call_target="tpu_custom_call" | custom-call | tf_op jit(solution)/shard_map/pallas_call | solution.py:379
  141.6 1.6 collective-permute-start.10
  146.6 7.6 %shard_map.95 = (bf16[2,1024,256]{2,1,0:T(8,128)(2,1)}, bf16[2,1024,256]{2,1,0:T(8,128)(2,1)}) custom-call(s32[12]{0:T(128)} %stack.58.table_ref, bf16[2048,512]{1,0:T(8,128)(2,1)} %get-tuple-element.32.own_ref, bf16[2048,512]{1,0:T(8,128)(2,1)} %copy-done, bf16[2,512,256]{2,1,0:T(8,128)(2,1)} %copy-done.1, bf16[2,512,256]{2,1,0:T(8,128)(2,1)} %copy-done.5, ...), custom_call_target="tpu_custom_call" | custom-call | tf_op jit(solution)/shard_map/pallas_call | solution.py:379
  154.2 21.5 %collective-permute-done.10 = bf16[1024,256]{1,0:T(8,128)(2,1)} collective-permute-done((bf16[1024,256]{1,0:T(8,128)(2,1)S(1)}, bf16[1024,256]{1,0:T(8,128)(2,1)}, u32[]{:S(2)}, u32[]{:S(2)}) %collective-permute-start.10) | collective-permute-done | bytes 524320 | tf_op jit(solution)/shard_map/ppermute | solution.py:393
  179.8 2.0 fusion.7
  183.3 11.6 %project.3.grad_ref = bf16[512,2048]{1,0:T(8,128)(2,1)} custom-call(s32[12]{0:T(128)} %stack.58.table_ref, bf16[2,512,256]{2,1,0:T(8,128)(2,1)} %copy-done.1, bf16[2,512,256]{2,1,0:T(8,128)(2,1)} %copy-done.5, bf16[2,512,256]{2,1,0:T(8,128)(2,1)} %copy-done.3, bf16[2,512,256]{2,1,0:T(8,128)(2,1)} %copy-done.6, bf16[2,512,256]{2,1,0:T(8,128)(2,1)} %copy-done.4, ...), custom_call_target="tpu_custom_call" | custom-call | tf_op jit(solution)/shard_map/project/pallas_call | solution.py:297
  194.9 6.8 %pulls.1 = (bf16[512,2048]{1,0:T(8,128)(2,1)}, f32[256,1024]{1,0:T(8,128)}) custom-call(bf16[512,2048]{1,0:T(8,128)(2,1)} %project.3.grad_ref, bf16[512,256]{1,0:T(8,128)(2,1)} %bitcast.52, f32[32,512]{1,0:T(8,128)} %bitcast.57), custom_call_target="tpu_custom_call" | custom-call | tf_op jit(solution)/shard_map/pulls/pallas_call | solution.py:484
  201.7 1.6 collective-permute-start.21
  209.8 9.3 %grads.1 = (bf16[512,2048]{1,0:T(8,128)(2,1)}, bf16[512,256]{1,0:T(8,128)(2,1)}, bf16[512,256]{1,0:T(8,128)(2,1)}) custom-call(bf16[512,2048]{1,0:T(8,128)(2,1)} %get-tuple-element.48.grad_ref, bf16[512,2048]{1,0:T(8,128)(2,1)} %get-tuple-element.30.scaled_ref, bf16[512,256]{1,0:T(8,128)(2,1)} %bitcast.50, bf16[512,256]{1,0:T(8,128)(2,1)} %bitcast.53, ...), custom_call_target="tpu_custom_call" | custom-call | tf_op jit(solution)/shard_map/grads/pallas_call | solution.py:486
  (77 shorter events, 32.4 us)
Async XLA Ops:
  1.9 2.0 collective-permute-start
  11.6 4.5 %collective-permute-start.1 = (f32[256,1024]{1,0:T(8,128)}, f32[256,1024]{1,0:T(8,128)S(1)}, u32[]{:S(2)}, u32[]{:S(2)}) collective-permute-start(f32[256,1024]{1,0:T(8,128)} %get-tuple-element.31), channel_id=1, source_target_pairs={{0,4},{1,5},{2,6},{3,7},{8,12},{9,13},{10,14},{11,15},{16,20},{17,... | collective-permute-start | bytes 3145736 | tf_op jit(solution)/shard_map/ppermute | solution.py:231
  24.4 43.9 %collective-permute-start.2 = (bf16[2048,512]{1,0:T(8,128)(2,1)}, bf16[2048,512]{1,0:T(8,128)(2,1)S(1)}, u32[]{:S(2)}, u32[]{:S(2)}) collective-permute-start(bf16[2048,512]{1,0:T(8,128)(2,1)} %get-tuple-element.32.own_ref), channel_id=1, source_target_pairs={{0,4},{4,0},{1,5},{5,1},{2,6},{6,2},{3,7},{7,3},{8,12},{12,8},{9,1... | collective-permute-start | bytes 6291464 | tf_op jit(solution)/shard_map/ppermute | solution.py:393
  26.0 42.3 %copy-start.2 = (bf16[2,512,256]{2,1,0:T(8,128)(2,1)}, bf16[2,512,256]{2,1,0:T(8,128)(2,1)S(1)}, u32[]{:S(2)}) copy-start(bf16[2,512,256]{2,1,0:T(8,128)(2,1)S(1)} %get-tuple-element.54.zero_ref) | copy-start | bytes 1572868
  26.0 90.1 %copy-start.1 = (bf16[2,512,256]{2,1,0:T(8,128)(2,1)}, bf16[2,512,256]{2,1,0:T(8,128)(2,1)S(1)}, u32[]{:S(2)}) copy-start(bf16[2,512,256]{2,1,0:T(8,128)(2,1)S(1)} %get-tuple-element.39.zero_ref) | copy-start | bytes 1572868
  26.1 26.3 %collective-permute-start.4 = (bf16[2,512,256]{2,1,0:T(8,128)(2,1)S(1)}, bf16[2,512,256]{2,1,0:T(8,128)(2,1)}, u32[]{:S(2)}, u32[]{:S(2)}) collective-permute-start(bf16[2,512,256]{2,1,0:T(8,128)(2,1)S(1)} %get-tuple-element.54.zero_ref), channel_id=1, source_target_pairs={{0,2},{1,3},{2,0},{3,1},{4,6},{5,7},{6,4},{7,5},{8,10},{9,11},{10,... | collective-permute-start | bytes 1572872 | tf_op jit(solution)/shard_map/ppermute | solution.py:393
  26.5 27.8 %collective-permute-start.5 = (bf16[2,512,256]{2,1,0:T(8,128)(2,1)S(1)}, bf16[2,512,256]{2,1,0:T(8,128)(2,1)}, u32[]{:S(2)}, u32[]{:S(2)}) collective-permute-start(bf16[2,512,256]{2,1,0:T(8,128)(2,1)S(1)} %get-tuple-element.54.zero_ref), channel_id=1, source_target_pairs={{1,2},{2,1},{5,6},{6,5},{9,10},{10,9},{13,14},{14,13},{17,18},{18,... | collective-permute-start | bytes 1572872 | tf_op jit(solution)/shard_map/ppermute | solution.py:411
  27.9 26.5 %collective-permute-start.3 = (bf16[2,512,256]{2,1,0:T(8,128)(2,1)S(1)}, bf16[2,512,256]{2,1,0:T(8,128)(2,1)}, u32[]{:S(2)}, u32[]{:S(2)}) collective-permute-start(bf16[2,512,256]{2,1,0:T(8,128)(2,1)S(1)} %get-tuple-element.54.zero_ref), channel_id=1, source_target_pairs={{0,1},{1,0},{2,3},{3,2},{4,5},{5,4},{6,7},{7,6},{8,9},{9,8},{10,11... | collective-permute-start | bytes 1572872 | tf_op jit(solution)/shard_map/ppermute | solution.py:393
  52.3 16.0 %collective-permute-start.6 = (bf16[2,512,256]{2,1,0:T(8,128)(2,1)}, bf16[2,512,256]{2,1,0:T(8,128)(2,1)}, u32[]{:S(2)}, u32[]{:S(2)}) collective-permute-start(bf16[2,512,256]{2,1,0:T(8,128)(2,1)} %collective-permute-done.4.two_ref), channel_id=1, source_target_pairs={{1,0},{2,3},{5,4},{6,7},{9,8},{10,11},{13,12},{14,15},{17,16},{18,... | collective-permute-start | bytes 1572872 | tf_op jit(solution)/shard_map/ppermute | solution.py:410
  77.6 30.4 %collective-permute-start.15 = (bf16[4,512,256]{2,1,0:T(8,128)(2,1)}, bf16[4,512,256]{2,1,0:T(8,128)(2,1)}, u32[]{:S(2)}, u32[]{:S(2)}) collective-permute-start(bf16[4,512,256]{2,1,0:T(8,128)(2,1)} %get-tuple-element.41), channel_id=1, source_target_pairs={{0,4},{4,0},{1,5},{5,1},{2,6},{6,2},{3,7},{7,3},{8,12},{12,8},{9,1... | collective-permute-start | bytes 3145736 | tf_op jit(solution)/shard_map/ppermute | solution.py:393
  77.7 25.4 %collective-permute-start.12 = (bf16[2,512,256]{2,1,0:T(8,128)(2,1)S(1)}, bf16[2,512,256]{2,1,0:T(8,128)(2,1)S(1)}, u32[]{:S(2)}, u32[]{:S(2)}) collective-permute-start(bf16[2,512,256]{2,1,0:T(8,128)(2,1)S(1)} %get-tuple-element.39.zero_ref), channel_id=1, source_target_pairs={{0,2},{1,3},{2,0},{3,1},{4,6},{5,7},{6,4},{7,5},{8,10},{9,11},{10,... | collective-permute-start | bytes 1572872 | tf_op jit(solution)/shard_map/ppermute | solution.py:393
  77.7 62.5 %collective-permute-start.9 = (bf16[2,1024,256]{2,1,0:T(8,128)(2,1)}, bf16[2,1024,256]{2,1,0:T(8,128)(2,1)}, u32[]{:S(2)}, u32[]{:S(2)}) collective-permute-start(bf16[2,1024,256]{2,1,0:T(8,128)(2,1)} %get-tuple-element.37), channel_id=1, source_target_pairs={{0,16},{8,24},{16,0},{24,8},{1,17},{9,25},{17,1},{25,9},{2,18},{10... | collective-permute-start | bytes 3145736 | tf_op jit(solution)/shard_map/ppermute | solution.py:393
  103.1 23.8 %collective-permute-start.14 = (bf16[2,512,256]{2,1,0:T(8,128)(2,1)S(1)}, bf16[2,512,256]{2,1,0:T(8,128)(2,1)S(1)}, u32[]{:S(2)}, u32[]{:S(2)}) collective-permute-start(bf16[2,512,256]{2,1,0:T(8,128)(2,1)S(1)} %collective-permute-done.12.two_ref), channel_id=1, source_target_pairs={{1,0},{2,3},{5,4},{6,7},{9,8},{10,11},{13,12},{14,15},{17,16},{18,... | collective-permute-start | bytes 1572872 | tf_op jit(solution)/shard_map/ppermute | solution.py:410
  104.4 25.7 %collective-permute-start.11 = (bf16[2,512,256]{2,1,0:T(8,128)(2,1)S(1)}, bf16[2,512,256]{2,1,0:T(8,128)(2,1)S(1)}, u32[]{:S(2)}, u32[]{:S(2)}) collective-permute-start(bf16[2,512,256]{2,1,0:T(8,128)(2,1)S(1)} %get-tuple-element.39.zero_ref), channel_id=1, source_target_pairs={{0,1},{1,0},{2,3},{3,2},{4,5},{5,4},{6,7},{7,6},{8,9},{9,8},{10,11... | collective-permute-start | bytes 1572872 | tf_op jit(solution)/shard_map/ppermute | solution.py:393
  107.1 23.0 %collective-permute-start.13 = (bf16[2,512,256]{2,1,0:T(8,128)(2,1)S(1)}, bf16[2,512,256]{2,1,0:T(8,128)(2,1)S(1)}, u32[]{:S(2)}, u32[]{:S(2)}) collective-permute-start(bf16[2,512,256]{2,1,0:T(8,128)(2,1)S(1)} %get-tuple-element.39.zero_ref), channel_id=1, source_target_pairs={{1,2},{2,1},{5,6},{6,5},{9,10},{10,9},{13,14},{14,13},{17,18},{18,... | collective-permute-start | bytes 1572872 | tf_op jit(solution)/shard_map/ppermute | solution.py:411
  108.0 36.7 %collective-permute-start.7 = (bf16[2,1024,256]{2,1,0:T(8,128)(2,1)}, bf16[2,1024,256]{2,1,0:T(8,128)(2,1)}, u32[]{:S(2)}, u32[]{:S(2)}) collective-permute-start(bf16[2,1024,256]{2,1,0:T(8,128)(2,1)} %get-tuple-element.35), channel_id=1, source_target_pairs={{0,8},{8,0},{16,24},{24,16},{1,9},{9,1},{17,25},{25,17},{2,10},{10... | collective-permute-start | bytes 3145736 | tf_op jit(solution)/shard_map/ppermute | solution.py:393
  139.7 37.5 %collective-permute-start.16 = (bf16[2,1024,256]{2,1,0:T(8,128)(2,1)}, bf16[2,1024,256]{2,1,0:T(8,128)(2,1)S(1)}, u32[]{:S(2)}, u32[]{:S(2)}) collective-permute-start(bf16[2,1024,256]{2,1,0:T(8,128)(2,1)} %get-tuple-element.44), channel_id=1, source_target_pairs={{0,8},{8,0},{16,24},{24,16},{1,9},{9,1},{17,25},{25,17},{2,10},{10... | collective-permute-start | bytes 3145736 | tf_op jit(solution)/shard_map/ppermute | solution.py:393
  141.6 34.1 %collective-permute-start.10 = (bf16[1024,256]{1,0:T(8,128)(2,1)S(1)}, bf16[1024,256]{1,0:T(8,128)(2,1)}, u32[]{:S(2)}, u32[]{:S(2)}) collective-permute-start(bf16[1024,256]{1,0:T(8,128)(2,1)S(1)} %fusion.5), channel_id=1, source_target_pairs={{0,8},{8,0},{16,24},{24,16},{1,9},{9,1},{17,25},{25,17},{2,10},{10... | collective-permute-start | bytes 1572872 | tf_op jit(solution)/shard_map/ppermute | solution.py:393
  143.2 36.7 %collective-permute-start.18 = (bf16[2,1024,256]{2,1,0:T(8,128)(2,1)}, bf16[2,1024,256]{2,1,0:T(8,128)(2,1)}, u32[]{:S(2)}, u32[]{:S(2)}) collective-permute-start(bf16[2,1024,256]{2,1,0:T(8,128)(2,1)} %get-tuple-element.46), channel_id=1, source_target_pairs={{0,16},{8,24},{16,0},{24,8},{1,17},{9,25},{17,1},{25,9},{2,18},{10... | collective-permute-start | bytes 3145736 | tf_op jit(solution)/shard_map/ppermute | solution.py:393
  144.7 37.7 %collective-permute-start.20 = (bf16[4,512,256]{2,1,0:T(8,128)(2,1)}, bf16[4,512,256]{2,1,0:T(8,128)(2,1)S(1)}, u32[]{:S(2)}, u32[]{:S(2)}) collective-permute-start(bf16[4,512,256]{2,1,0:T(8,128)(2,1)} %get-tuple-element.47), channel_id=1, source_target_pairs={{0,4},{4,0},{1,5},{5,1},{2,6},{6,2},{3,7},{7,3},{8,12},{12,8},{9,1... | collective-permute-start | bytes 3145736 | tf_op jit(solution)/shard_map/ppermute | solution.py:393
  146.0 57.3 %collective-permute-start.8 = (bf16[1024,256]{1,0:T(8,128)(2,1)S(1)}, bf16[1024,256]{1,0:T(8,128)(2,1)}, u32[]{:S(2)}, u32[]{:S(2)}) collective-permute-start(bf16[1024,256]{1,0:T(8,128)(2,1)S(1)} %fusion.4), channel_id=1, source_target_pairs={{0,16},{8,24},{16,0},{24,8},{1,17},{9,25},{17,1},{25,9},{2,18},{10... | collective-permute-start | bytes 1572872 | tf_op jit(solution)/shard_map/ppermute | solution.py:393
  178.3 26.4 %collective-permute-start.17 = (bf16[1024,256]{1,0:T(8,128)(2,1)}, bf16[1024,256]{1,0:T(8,128)(2,1)}, u32[]{:S(2)}, u32[]{:S(2)}) collective-permute-start(bf16[1024,256]{1,0:T(8,128)(2,1)} %fusion.6), channel_id=1, source_target_pairs={{0,16},{8,24},{16,0},{24,8},{1,17},{9,25},{17,1},{25,9},{2,18},{10... | collective-permute-start | bytes 1572872 | tf_op jit(solution)/shard_map/ppermute | solution.py:393
  181.8 24.2 %collective-permute-start.19 = (bf16[1024,256]{1,0:T(8,128)(2,1)}, bf16[1024,256]{1,0:T(8,128)(2,1)}, u32[]{:S(2)}, u32[]{:S(2)}) collective-permute-start(bf16[1024,256]{1,0:T(8,128)(2,1)} %fusion.7), channel_id=1, source_target_pairs={{0,8},{8,0},{16,24},{24,16},{1,9},{9,1},{17,25},{25,17},{2,10},{10... | collective-permute-start | bytes 1572872 | tf_op jit(solution)/shard_map/ppermute | solution.py:393
  201.7 7.1 %collective-permute-start.21 = (f32[256,1024]{1,0:T(8,128)}, f32[256,1024]{1,0:T(8,128)S(1)}, u32[]{:S(2)}, u32[]{:S(2)}) collective-permute-start(f32[256,1024]{1,0:T(8,128)} %get-tuple-element.50), channel_id=1, source_target_pairs={{4,0},{5,1},{6,2},{7,3},{12,8},{13,9},{14,10},{15,11},{20,16},{21,... | collective-permute-start | bytes 3145736 | tf_op jit(solution)/shard_map/ppermute | solution.py:231
  (15 other events, 94.7 us)

commit v2 on v1

v2 whole, which is shorter than its diff:
```python
import functools

import jax
import jax.numpy as jnp
from jax import lax
from jax.experimental import pallas as pl
from jax.experimental.pallas import tpu as pltpu
from jax.sharding import PartitionSpec as P


HEAD_DIM = 64
STATE = 128
CHUNK = 128
LANES = 128
PER_STEP = 2
FINISH_STEPS = 2
PARTS = 2
THIS_MESH = (4, 2, 4)

BF16 = jnp.bfloat16
F32 = jnp.float32


def dot(a, b, dims):
    return lax.dot_general(a, b, (dims, ((), ())), preferred_element_type=F32)


NN = ((1,), (0,))
NT = ((1,), (1,))
TN = ((0,), (0,))


def causal_mask():
    rows = lax.broadcasted_iota(jnp.int32, (CHUNK, CHUNK), 0)
    cols = lax.broadcasted_iota(jnp.int32, (CHUNK, CHUNK), 1)
    return rows >= cols


def chunk_decays(decays):
    ones = jnp.where(causal_mask(), 1.0, 0.0).astype(BF16)
    first = decays.astype(BF16)
    rest = decays - first.astype(F32)
    second = rest.astype(BF16)
    third = (rest - second.astype(F32)).astype(BF16)
    running = dot(ones, first, NT) + dot(ones, second, NT) + dot(ones, third, NT)
    half = 0.5 * running[CHUNK - 1 : CHUNK, :]
    return jnp.exp(running - half), jnp.exp(half - running), jnp.exp(half)


def over_columns(factors, block):
    rows = factors.shape[0]
    per_block = LANES // HEAD_DIM
    lanes = lax.broadcasted_iota(jnp.int32, (rows, LANES), 1)
    head = block * per_block
    return jnp.where(
        lanes < HEAD_DIM,
        jnp.broadcast_to(factors[:, head : head + 1], (rows, LANES)),
        jnp.broadcast_to(factors[:, head + 1 : head + 2], (rows, LANES)),
    )


def over_group(factors, group, width):
    blocks = width // LANES
    return jnp.concatenate(
        [over_columns(factors, group * blocks + i) for i in range(blocks)], axis=1
    )


def states_kernel(x_ref, b_ref, decay_ref, scaled_ref, state_ref, *, groups):
    width = x_ref.shape[1] // groups

    @pl.when(pl.program_id(0) == 0)
    def _():
        state_ref[...] = jnp.zeros_like(state_ref)

    for c in range(x_ref.shape[0] // CHUNK):
        now = slice(c * CHUNK, (c + 1) * CHUNK)
        _, shrink, half = chunk_decays(decay_ref[:, now])
        for g in range(groups):
            cols = slice(g * width, (g + 1) * width)
            rows = slice(g * STATE, (g + 1) * STATE)
            scaled = (x_ref[now, cols].astype(F32) * over_group(shrink, g, width)).astype(BF16)
            scaled_ref[now, cols] = scaled
            halves = over_group(half, g, width)
            added = dot(b_ref[now, rows], scaled, TN)
            state_ref[rows, :] = halves * (halves * state_ref[rows, :] + added)


def scan_kernel(
    scaled_ref, b_ref, c_ref, decay_ref, enter_ref, rows_ref, held_ref, state_ref, *, groups
):
    width = scaled_ref.shape[1] // groups

    @pl.when(pl.program_id(0) == 0)
    def _():
        state_ref[...] = enter_ref[...]

    mask = causal_mask()
    for c in range(scaled_ref.shape[0] // CHUNK):
        now = slice(c * CHUNK, (c + 1) * CHUNK)
        grow, _, half = chunk_decays(decay_ref[:, now])
        for g in range(groups):
            cols = slice(g * width, (g + 1) * width)
            rows = slice(g * STATE, (g + 1) * STATE)
            scaled = scaled_ref[now, cols]
            writes = b_ref[now, rows]
            reads = c_ref[now, rows]
            halves = over_group(half, g, width)
            held = halves * state_ref[rows, :]
            held_low = held.astype(BF16)
            held_ref[c, rows, :] = held_low
            affinity = jnp.where(mask, dot(reads, writes, NT), 0.0).astype(BF16)
            out = dot(affinity, scaled, NN) + dot(reads, held_low, NN)
            out = out * over_group(grow, g, width)
            rows_ref[cols, now] = out.T.astype(BF16)
            state_ref[rows, :] = halves * (held + dot(writes, scaled, TN))


def pulls_kernel(grad_ref, c_ref, decay_ref, scaled_ref, state_ref, *, groups):
    width = grad_ref.shape[1] // groups

    @pl.when(pl.program_id(0) == 0)
    def _():
        state_ref[...] = jnp.zeros_like(state_ref)

    for c in reversed(range(grad_ref.shape[0] // CHUNK)):
        now = slice(c * CHUNK, (c + 1) * CHUNK)
        grow, _, half = chunk_decays(decay_ref[:, now])
        for g in range(groups):
            cols = slice(g * width, (g + 1) * width)
            rows = slice(g * STATE, (g + 1) * STATE)
            scaled = (grad_ref[now, cols].astype(F32) * over_group(grow, g, width)).astype(BF16)
            scaled_ref[now, cols] = scaled
            halves = over_group(half, g, width)
            pulled = dot(c_ref[now, rows], scaled, TN)
            state_ref[rows, :] = halves * (halves * state_ref[rows, :] + pulled)


def grads_kernel(
    grad_ref, scaled_ref, b_ref, c_ref, decay_ref, held_ref, leave_ref,
    x_grad_ref, b_grad_ref, c_grad_ref, state_ref, *, groups,
):
    width = grad_ref.shape[1] // groups

    @pl.when(pl.program_id(0) == 0)
    def _():
        state_ref[...] = leave_ref[...]

    mask = causal_mask()
    for c in reversed(range(grad_ref.shape[0] // CHUNK)):
        now = slice(c * CHUNK, (c + 1) * CHUNK)
        _, shrink, half = chunk_decays(decay_ref[:, now])
        for g in range(groups):
            cols = slice(g * width, (g + 1) * width)
            rows = slice(g * STATE, (g + 1) * STATE)
            grad = grad_ref[now, cols]
            scaled = scaled_ref[now, cols]
            writes = b_ref[now, rows]
            reads = c_ref[now, rows]
            halves = over_group(half, g, width)
            left = halves * state_ref[rows, :]
            left_low = left.astype(BF16)
            affinity = jnp.where(mask, dot(reads, writes, NT), 0.0).astype(BF16)
            x_grad = dot(affinity, grad, TN) + dot(writes, left_low, NN)
            x_grad_ref[now, cols] = (x_grad * over_group(shrink, g, width)).astype(BF16)
            pair = jnp.where(mask, dot(grad, scaled, NT), 0.0).astype(BF16)
            c_grad = dot(pair, writes, NN) + dot(grad, held_ref[c, rows, :], NT)
            c_grad_ref[now, rows] = c_grad.astype(BF16)
            b_grad = dot(pair, reads, TN) + dot(scaled, left_low, NT)
            b_grad_ref[now, rows] = b_grad.astype(BF16)
            state_ref[rows, :] = halves * (left + dot(reads, grad, TN))


def scan_calls(tokens, heads, groups):
    inner = heads * HEAD_DIM
    width = inner // groups
    keys = groups * STATE
    chunks = tokens // CHUNK
    per_step = PER_STEP if chunks % PER_STEP == 0 else 1
    steps = chunks // per_step
    tall = per_step * CHUNK
    call = functools.partial(pl.pallas_call, grid=(steps,))

    def ahead(cols):
        return pl.BlockSpec((tall, cols), lambda i: (i, 0))

    def back(cols):
        return pl.BlockSpec((tall, cols), lambda i: (steps - 1 - i, 0))

    decays_ahead = pl.BlockSpec((heads, tall), lambda i: (0, i))
    decays_back = pl.BlockSpec((heads, tall), lambda i: (0, steps - 1 - i))
    whole = pl.BlockSpec((keys, width), lambda i: (0, 0))
    state_type = jax.ShapeDtypeStruct((keys, width), F32)
    rows_type = jax.ShapeDtypeStruct((tokens, inner), BF16)
    keys_type = jax.ShapeDtypeStruct((tokens, keys), BF16)
    held_type = jax.ShapeDtypeStruct((chunks, keys, width), BF16)
    scratch = [pltpu.VMEM((keys, width), F32)]
    states = call(
        functools.partial(states_kernel, groups=groups),
        in_specs=[ahead(inner), ahead(keys), decays_ahead],
        out_specs=[ahead(inner), whole],
        out_shape=[rows_type, state_type],
        name="states",
    )
    scan = call(
        functools.partial(scan_kernel, groups=groups),
        in_specs=[ahead(inner), ahead(keys), ahead(keys), decays_ahead, whole],
        out_specs=[
            pl.BlockSpec((inner, tall), lambda i: (0, i)),
            pl.BlockSpec((per_step, keys, width), lambda i: (i, 0, 0)),
        ],
        out_shape=[jax.ShapeDtypeStruct((inner, tokens), BF16), held_type],
        scratch_shapes=scratch,
        name="scan",
    )
    pulls = call(
        functools.partial(pulls_kernel, groups=groups),
        in_specs=[back(inner), back(keys), decays_back],
        out_specs=[back(inner), whole],
        out_shape=[rows_type, state_type],
        name="pulls",
    )
    grads = call(
        functools.partial(grads_kernel, groups=groups),
        in_specs=[
            back(inner), back(inner), back(keys), back(keys), decays_back,
            pl.BlockSpec((per_step, keys, width), lambda i: (steps - 1 - i, 0, 0)), whole,
        ],
        out_specs=[back(inner), back(keys), back(keys)],
        out_shape=[rows_type, keys_type, keys_type],
        scratch_shapes=scratch,
        name="grads",
    )
    return states, scan, pulls, grads


def passed_along(shard, axis, by):
    length = lax.axis_size(axis)
    pairs = [(i, i + by) for i in range(length) if 0 <= i + by < length]
    return lax.ppermute(shard, axis, pairs)


def chained(local, log_decay, groups, axis, by):
    incoming = passed_along(local, axis, by)
    turns = lax.axis_size(axis) - 1
    if turns > 1:
        total = jnp.exp(jnp.sum(log_decay, axis=1)).reshape(groups, 1, -1)
        spread = jnp.repeat(total, HEAD_DIM, axis=2)
        spread = jnp.broadcast_to(spread, (groups, STATE, spread.shape[2]))
        spread = spread.reshape(local.shape)

        def turn(_, arrived):
            return passed_along(spread * arrived + local, axis, by)

        incoming = lax.fori_loop(0, turns - 1, turn, incoming)
    return incoming


def any_mesh(rows_t, out_grad, out_weight):
    full = lax.all_gather(out_grad, "tensor", axis=1, tiled=True)
    y_grad = lax.dot_general(
        full, out_weight, (NT, ((), ())), preferred_element_type=F32
    ).astype(BF16)
    part = lax.dot_general(rows_t, full, (NN, ((), ())), preferred_element_type=F32)
    weight_grad = lax.psum_scatter(
        part.astype(BF16), ("dp", "seq"), scatter_dimension=1, tiled=True
    )
    return y_grad, weight_grad


def project_kernel(table_ref, *refs, blocks, first, flip):
    step = pl.program_id(0)
    low_ref, high_ref = refs[-4:-2]
    out_ref, total_ref = refs[-2:]
    sources = refs[:-4] if first else refs[:-5]
    steps = len(blocks) // 2
    for i in range(steps):

        @pl.when(step == i)
        def _():
            low, high = (pick(sources) for pick in blocks[2 * i : 2 * i + 2])
            got = dot(low_ref[...], low, NT) + dot(high_ref[...], high, NT)
            if i > 0:
                got += total_ref[...]
            elif not first:
                got += refs[-5][...]
            if i < steps - 1:
                total_ref[...] = got
            elif flip:
                out_ref[...] = got.T.astype(out_ref.dtype)
            else:
                out_ref[...] = got


def project(table, at, sources, blocks, out_weight, wide, before, flip):
    tokens = sources[0].shape[-2]
    inner = out_weight.shape[0]
    whole = pl.BlockSpec((inner, tokens), lambda i, t: (0, 0))
    flipped = pl.BlockSpec((tokens, inner), lambda i, t: (0, 0))

    def held(source):
        return pl.BlockSpec(source.shape, lambda i, t: (0,) * source.ndim)

    given = [] if before is None else [before]
    return pl.pallas_call(
        functools.partial(project_kernel, blocks=blocks, first=before is None, flip=flip),
        grid_spec=pltpu.PrefetchScalarGridSpec(
            num_scalar_prefetch=1,
            grid=(len(blocks) // 2,),
            in_specs=[held(source) for source in sources]
            + [whole] * len(given)
            + [
                pl.BlockSpec((inner, wide), lambda i, t: (0, t[at + 2 * i])),
                pl.BlockSpec((inner, wide), lambda i, t: (0, t[at + 2 * i + 1])),
            ],
            out_specs=flipped if flip else whole,
            scratch_shapes=[pltpu.VMEM((inner, tokens), F32)],
        ),
        out_shape=jax.ShapeDtypeStruct(*(((tokens, inner), BF16) if flip else ((inner, tokens), F32))),
        name="project",
    )(table, *sources, *given, out_weight, out_weight)


def partial_kernel(
    table_ref, own_ref, other_ref, zero_ref, one_ref, two_ref, mid_ref, end_ref,
    x_send_ref, y_send_ref, x_keep_ref, y_keep_ref, rest_ref, last_ref, picked_ref,
):
    step = pl.program_id(0)
    half_steps = pl.num_programs(0) // 2
    wide = zero_ref.shape[2]

    @pl.when(step == 0)
    def _():
        last = mid_ref[...] + end_ref[...]
        last_ref[...] = last[0]
        rest_ref[0] = one_ref[1]
        rest_ref[1] = two_ref[1]
        rest_ref[2] = last[1]
        for target in range(4):
            cols = slice(target * wide, (target + 1) * wide)
            slot = table_ref[target]
            for q, ref in enumerate((zero_ref, one_ref, two_ref)):

                @pl.when(slot == q)
                def _():
                    picked_ref[:, :, cols] = ref[...]

            @pl.when(slot == 3)
            def _():
                picked_ref[:, :, cols] = last

    def put(*places):
        for target, (ref, place) in enumerate(places):
            cols = slice(target * wide, (target + 1) * wide)
            got = dot(own_ref[...], picked_ref[0, :, cols], NN)
            got += dot(other_ref[...], picked_ref[1, :, cols], NN)
            ref[place] = got.astype(BF16)

    @pl.when(step < half_steps)
    def _():
        put((x_keep_ref, 0), (x_send_ref, 0), (x_keep_ref, 1), (x_send_ref, 1))

    @pl.when(step >= half_steps)
    def _():
        put((y_keep_ref, 0), (y_keep_ref, 1), (y_send_ref, 0), (y_send_ref, 1))


def partials(table, own, other, slots):
    inner, tokens = own.shape
    wide = slots[0].shape[2]
    steps = 4
    tall = inner // steps
    half_steps = steps // 2
    rows = pl.BlockSpec((tall, tokens), lambda i, t: (i, 0))
    held = pl.BlockSpec((2, tokens, wide), lambda i, t: (0, 0, 0))
    out_type = jax.ShapeDtypeStruct((2, inner // 2, wide), BF16)
    upper = pl.BlockSpec((2, tall, wide), lambda i, t: (0, jnp.minimum(i, half_steps - 1), 0))
    lower = pl.BlockSpec((2, tall, wide), lambda i, t: (0, jnp.maximum(i - half_steps, 0), 0))
    return pl.pallas_call(
        partial_kernel,
        grid_spec=pltpu.PrefetchScalarGridSpec(
            num_scalar_prefetch=1,
            grid=(steps,),
            in_specs=[rows, rows] + [held] * 5,
            out_specs=[
                upper, lower, upper, lower,
                pl.BlockSpec((3, tokens, wide), lambda i, t: (0, 0, 0)),
                pl.BlockSpec((tokens, wide), lambda i, t: (0, 0)),
            ],
            scratch_shapes=[pltpu.VMEM((2, tokens, 4 * wide), BF16)],
        ),
        out_shape=[out_type] * 4
        + [
            jax.ShapeDtypeStruct((3, tokens, wide), BF16),
            jax.ShapeDtypeStruct((tokens, wide), BF16),
        ],
        name="partials",
    )(table, own, other, *slots)


def finish_kernel(x_keep_ref, x_got_ref, x_last_ref, y_keep_ref, y_got_ref, y_last_ref, *refs):
    out_ref = refs[-1]

    def put(place, keep_ref, got_ref, last_ref):
        summed = keep_ref[0].astype(F32) + got_ref[0].astype(F32) + last_ref[...].astype(F32)
        out_ref[place] = summed.astype(BF16)

    put(0, x_keep_ref, x_got_ref, x_last_ref)
    put(1, y_keep_ref, y_got_ref, y_last_ref)


def finish(x_terms, y_terms, part, parts, before):
    half, wide = x_terms[2].shape
    steps = FINISH_STEPS
    tall = half // steps
    specs = [
        pl.BlockSpec((1, tall, wide), lambda i: (0, i, 0)),
        pl.BlockSpec((1, tall, wide), lambda i: (0, i, 0)),
        pl.BlockSpec((tall, wide), lambda i: (i, 0)),
    ]
    given = [] if before is None else [before]
    return pl.pallas_call(
        finish_kernel,
        grid=(steps,),
        in_specs=specs * 2 + [pl.BlockSpec(memory_space=pl.ANY)] * len(given),
        out_specs=pl.BlockSpec((2, tall, wide), lambda i: (0, i, part)),
        out_shape=jax.ShapeDtypeStruct((2, half, parts * wide), BF16),
        input_output_aliases={6: 0} if given else {},
        name="finish",
    )(*x_terms, *y_terms, *given)


def swapped(value, axis, by):
    return lax.ppermute(value, axis, [(i, i ^ by) for i in range(lax.axis_size(axis))])


def total(*terms):
    return functools.reduce(jnp.add, [t.astype(F32) for t in terms]).astype(BF16)


def after(value, *others):
    return lax.optimization_barrier((value, *others))[0]


def gathered(own, held_up):
    two = swapped(own, "tensor", 2)
    one = swapped(own, "tensor", 1)
    own_late, two_late = own, two
    if held_up:
        own_late, two_late = lax.optimization_barrier((own, two, *held_up))[:2]
    end = lax.ppermute(two_late, "tensor", [(1, 0), (2, 3)])
    mid = lax.ppermute(own_late, "tensor", [(1, 2), (2, 1)])
    return own, one, two, mid, end


def core_halves(out_grad):
    half = out_grad.shape[1] // 2
    core = lax.axis_index("seq")
    mine = lax.dynamic_slice_in_dim(out_grad, core * half, half, 1)
    theirs = lax.dynamic_slice_in_dim(out_grad, (1 - core) * half, half, 1)
    return jnp.stack([mine, swapped(theirs, "seq", 1)])


def this_mesh(rows_t, out_grad, both, out_weight):
    parts = PARTS
    wide = both.shape[2] // parts
    place = lax.axis_index("tensor")
    repo = lax.axis_index("dp")
    core = lax.axis_index("seq")

    def column(q, half, part):
        return ((place ^ q) * 2 + half) * parts + part

    mine, rest_half = core, 1 - core
    table = jnp.stack(
        [place ^ repo ^ r for r in range(4)]
        + [place * 4 + i for i in range(4)]
        + [column(q, mine, 0) for q in (1, 2)]
        + [column(q, rest_half, 0) for q in (1, 2, 3)]
        + [column(3, mine, 0)]
        + [column(q, mine, 1) for q in (1, 2, 3)]
        + [column(q, rest_half, 1) for q in (1, 2, 3)]
    ).astype(jnp.int32)
    other = swapped(rows_t, "seq", 1)
    y_grad = weight_grad = None
    ahead = late = None
    for part in range(parts):
        own = lax.slice_in_dim(both, part * wide, (part + 1) * wide, axis=2)
        if ahead is not None:
            own = after(own, *ahead)
        own, one, two, mid, end = gathered(own, late)
        ahead = (mid, end)
        if part == 0:
            blocks = [lambda r, i=i: r[0][:, i * wide : (i + 1) * wide] for i in range(4)]
            blocks += [lambda r: r[1][0], lambda r: r[2][0]]
            y_grad = project(table, 4, (out_grad, one, two), blocks, out_weight, wide, None, False)
        else:
            end = after(end, y_grad)
        x_send, y_send, x_keep, y_keep, rest, last = partials(
            table, rows_t, other, (own, one, two, mid, end)
        )
        late = (x_send,)
        x_got = swapped(x_send, "dp", 1)
        y_got = swapped(y_send, "dp", 2)
        rest = swapped(rest, "seq", 1)
        x_last = swapped(total(x_keep[1], x_got[1]), "dp", 2)
        y_last = swapped(total(y_keep[1], y_got[1]), "dp", 1)
        weight_grad = finish(
            (x_keep, x_got, x_last), (y_keep, y_got, y_last), part, parts, weight_grad
        )
        from_rest = [lambda r, i=i: r[0][i] for i in range(3)]
        if part == 0:
            y_grad = project(
                table, 10, (rest, last), from_rest + [lambda r: r[1][...]],
                out_weight, wide, y_grad, False,
            )
        else:
            blocks = [lambda r: r[1][0], lambda r: r[2][0], lambda r: r[3][...]]
            y_grad = project(
                table, 14, (rest, one, two, last), blocks + from_rest,
                out_weight, wide, y_grad, True,
            )
    return y_grad, weight_grad.reshape(-1, parts * wide)


def per_device(x_in, b_in, c_in, log_decay, out_weight, out_grad):
    x_in, b_in, c_in, log_decay, out_grad = (
        x_in[0], b_in[0], c_in[0], log_decay[0], out_grad[0],
    )
    tokens, heads = log_decay.shape
    log_decay = log_decay.T
    groups = b_in.shape[1] // STATE
    sizes = tuple(lax.axis_size(name) for name in ("dp", "seq", "tensor"))
    here = sizes == THIS_MESH
    if here:
        both = core_halves(out_grad)
        log_decay, both = lax.optimization_barrier((log_decay, both))
    states, scan, pulls, grads = scan_calls(tokens, heads, groups)
    scaled, end_local = states(x_in, b_in, log_decay)
    entering = chained(end_local, log_decay, groups, "seq", 1)
    rows_t, held = scan(scaled, b_in, c_in, log_decay, entering)
    if here:
        y_grad, weight_grad = this_mesh(rows_t, out_grad, both, out_weight)
    else:
        y_grad, weight_grad = any_mesh(rows_t, out_grad, out_weight)
    grad, start_local = pulls(y_grad, c_in, log_decay)
    leaving = chained(start_local, log_decay, groups, "seq", -1)
    x_grad, b_grad, c_grad = grads(grad, scaled, b_in, c_in, log_decay, held, leaving)
    return weight_grad, x_grad[None], b_grad[None], c_grad[None]


def solution(mesh):
    tokens_spec = P("dp", "seq", "tensor")

    program = jax.shard_map(
        per_device,
        mesh=mesh,
        in_specs=(tokens_spec,) * 4 + (P("tensor", None), tokens_spec),
        out_specs=(P("tensor", ("dp", "seq")),) + (tokens_spec,) * 3,
        check_vma=False,
    )
    if tuple(mesh.shape[name] for name in ("dp", "seq", "tensor")) != THIS_MESH:
        return program
    return program
```

time: 223 us -> 209 us (0.937)
  other arithmetic: 13.8 us -> 6.26 us
  waiting for transfers between devices: 87.6 us -> 84.6 us
  starting transfers between devices: 24.4 us -> 22.1 us
    convert_element_type x8 -> x4, other arithmetic: 11.2 us -> 6.16 us  [total(): functools.reduce(jnp.add, [t.astype(F32) for t in terms]).astype(BF16)]
    ppermute x16, waiting for transfers between devices: 71.4 us -> 68.4 us  [swapped(): lax.ppermute(value, axis, [(i, i ^ by) for i in range(lax.axis_size(axis))])]
    ppermute x16, starting transfers between devices: 15.9 us -> 13.2 us  [swapped(): lax.ppermute(value, axis, [(i, i ^ by) for i in range(lax.axis_size(axis))])]
    unnamed x34 -> x26, local copies, waits for them, and re-layouts: 5.89 us -> 4.9 us
    pallas_call x6 -> x7, Pallas kernels: 53.3 us -> 53.5 us  [the longest x3 27.5 us: project(): pl.pallas_call(functools.partial(project_kernel, blocks=blocks, first=bef...]
  transfers between devices with their start and end apart: 22 -> 22, of which waited for: 8 -> 10; matrix products, arithmetic and copies ran while one was open for 7% -> 4% of each run, Pallas kernels for 24% -> 24%
where the time goes in v2:
time: 209 us; the launch traced here: 206 us
  waiting for transfers between devices  84.6 us (40%)
  Pallas kernels  84.5 us (40%)
  starting transfers between devices  22.1 us (11%)
  local copies, waits for them, and re-layouts  7.87 us (4%)
  other arithmetic  6.26 us (3%)
    ppermute x16, waiting for transfers between devices, swapped(): lax.ppermute(value, axis, [(i, i ^ by) for i in range(lax.axis_size(axis))])  68.4 us
    pallas_call x3, Pallas kernels, project(): pl.pallas_call(functools.partial(project_kernel, blocks=blocks, first=bef...  27.5 us
    pallas_call x2, Pallas kernels, partials(): pl.pallas_call(partial_kernel, grid_spec=pltpu.PrefetchScalarGridSpec(num...  20.4 us
    ppermute x2, waiting for transfers between devices, gathered(): end = lax.ppermute(two_late, 'tensor', [(1, 0), (2, 3)])  13.8 us
    ppermute x16, starting transfers between devices, swapped(): lax.ppermute(value, axis, [(i, i ^ by) for i in range(lax.axis_size(axis))])  13.2 us
    pallas_call x1, Pallas kernels, per_device(): grads(grad, scaled, b_in, c_in, log_decay, held, leaving)  9.79 us
    pallas_call x1, Pallas kernels, per_device(): rows_t, held = scan(scaled, b_in, c_in, log_decay, entering)  7.76 us
    pallas_call x1, Pallas kernels, per_device(): grad, start_local = pulls(y_grad, c_in, log_decay)  6.91 us
  transfers between devices with their start and end apart: 22, of which 10 were waited for; matrix products, arithmetic and copies ran while one was open for 4% of the time, Pallas kernels for 24%

profile of v2, /device:TPU:26, one launch (start us, length us, event | category | flops | bytes accessed | tf_op | source)
XLA Modules:
  0.0 206.3 jit_solution(5853054386160752595)
XLA Ops:
  2.0 1.9 collective-permute-done
  4.0 6.6 %states.1 = (bf16[512,2048]{1,0:T(8,128)(2,1)}, f32[256,1024]{1,0:T(8,128)}) custom-call(bf16[512,2048]{1,0:T(8,128)(2,1)} %bitcast.50, bf16[512,256]{1,0:T(8,128)(2,1)} %bitcast.44, f32[32,512]{1,0:T(8,128)} %bitcast.51), custom_call_target="tpu_custom_call" | custom-call | tf_op jit(solution)/shard_map/states/pallas_call | solution.py:539
  10.6 2.1 %collective-permute-start.1 = (f32[256,1024]{1,0:T(8,128)}, f32[256,1024]{1,0:T(8,128)S(1)}, u32[]{:S(2)}, u32[]{:S(2)}) collective-permute-start(f32[256,1024]{1,0:T(8,128)} %get-tuple-element.33), channel_id=1, source_target_pairs={{0,4},{1,5},{2,6},{3,7},{8,12},{9,13},{10,14},{11,15},{16,20},{17,... | collective-permute-start | bytes 3145736 | tf_op jit(solution)/shard_map/ppermute | solution.py:240
  12.7 2.4 %collective-permute-done.1.enter_ref = f32[256,1024]{1,0:T(8,128)S(1)} collective-permute-done((f32[256,1024]{1,0:T(8,128)}, f32[256,1024]{1,0:T(8,128)S(1)}, u32[]{:S(2)}, u32[]{:S(2)}) %collective-permute-start.1) | collective-permute-done | bytes 1048608 | tf_op jit(solution)/shard_map/ppermute | solution.py:240
  16.1 7.8 %scan.1 = (bf16[2048,512]{1,0:T(8,128)(2,1)}, bf16[4,256,1024]{2,1,0:T(8,128)(2,1)}) custom-call(bf16[512,2048]{1,0:T(8,128)(2,1)} %get-tuple-element.32.scaled_ref, bf16[512,256]{1,0:T(8,128)(2,1)} %bitcast.45, bf16[512,256]{1,0:T(8,128)(2,1)} %bitcast.47, f32[32,512]{1,0:T(8,128)} %bitcast.52, f32[256,1024]{1,0:T(8,128)} %copy-done.9), custom_call_target="tpu_custom_call" | custom-call | tf_op jit(solution)/shard_map/scan/pallas_call | solution.py:541
  27.5 24.0 %collective-permute-done.4.two_ref.refs_2_ = bf16[2,512,256]{2,1,0:T(8,128)(2,1)S(1)} collective-permute-done((bf16[2,512,256]{2,1,0:T(8,128)(2,1)}, bf16[2,512,256]{2,1,0:T(8,128)(2,1)S(1)}, u32[]{:S(2)}, u32[]{:S(2)}) %collective-permute-start.4) | collective-permute-done | bytes 524320 | tf_op jit(solution)/shard_map/ppermute | solution.py:434
  53.5 13.8 %collective-permute-done.5.end_ref = bf16[2,512,256]{2,1,0:T(8,128)(2,1)} collective-permute-done((bf16[2,512,256]{2,1,0:T(8,128)(2,1)S(1)}, bf16[2,512,256]{2,1,0:T(8,128)(2,1)}, u32[]{:S(2)}, u32[]{:S(2)}) %collective-permute-start.5) | collective-permute-done | bytes 524320 | tf_op jit(solution)/shard_map/ppermute | solution.py:451
  68.6 10.2 %partials.2 = (bf16[2,1024,256]{2,1,0:T(8,128)(2,1)}, bf16[2,1024,256]{2,1,0:T(8,128)(2,1)}, bf16[2,1024,256]{2,1,0:T(8,128)(2,1)}, bf16[2,1024,256]{2,1,0:T(8,1...) custom-call(s32[20]{0:T(128)} %stack.90.table_ref, bf16[2048,512]{1,0:T(8,128)(2,1)} %get-tuple-element.34.own_ref, ...), custom_call_target="tpu_custom_call" | custom-call | tf_op jit(solution)/shard_map/partials/pallas_call | solution.py:379
  79.0 1.6 collective-permute-start.18
  80.6 24.0 %collective-permute-done.7.two_ref.refs_2_ = bf16[2,512,256]{2,1,0:T(8,128)(2,1)} collective-permute-done((bf16[2,512,256]{2,1,0:T(8,128)(2,1)}, bf16[2,512,256]{2,1,0:T(8,128)(2,1)}, u32[]{:S(2)}, u32[]{:S(2)}) %collective-permute-start.7) | collective-permute-done | bytes 524320 | tf_op jit(solution)/shard_map/ppermute | solution.py:434
  105.9 3.5 %collective-permute-start.6 = (bf16[2,512,256]{2,1,0:T(8,128)(2,1)}, bf16[2,512,256]{2,1,0:T(8,128)(2,1)}, u32[]{:S(2)}, u32[]{:S(2)}) collective-permute-start(bf16[2,512,256]{2,1,0:T(8,128)(2,1)} %get-tuple-element.38.zero_ref), channel_id=1, source_target_pairs={{0,1},{1,0},{2,3},{3,2},{4,5},{5,4},{6,7},{7,6},{8,9},{9,8},{10,11... | collective-permute-start | bytes 1572872 | tf_op jit(solution)/shard_map/ppermute | solution.py:434
  111.3 9.1 %project.3.refs_2_ = f32[2048,512]{1,0:T(8,128)} custom-call(s32[20]{0:T(128)} %stack.90.table_ref, bf16[512,1024]{1,0:T(8,128)(2,1)} %bitcast.43, bf16[2,512,256]{2,1,0:T(8,128)(2,1)} %copy-done.7, bf16[2,512,256]{2,1,0:T(8,128)(2,1)} %copy-done.6, bf16[2048,4096]{1,0:T(8,128)(2,1)} %refs_6_.1, bf16[2048,4096]{1,0:T(8,128)(2,1)} %refs_6_.1), custom_call_target="tpu_custom_call" | custom-call | tf_op jit(solution)/shard_map/project/pallas_call | solution.py:305
  120.4 8.5 %project.4.refs_4_ = f32[2048,512]{1,0:T(8,128)} custom-call(s32[20]{0:T(128)} %stack.90.table_ref, bf16[3,512,256]{2,1,0:T(8,128)(2,1)} %copy-done.10, bf16[512,256]{1,0:T(8,128)(2,1)} %get-tuple-element.41.refs_1_, f32[2048,512]{1,0:T(8,128)} %project.3.refs_2_, bf16[2048,4096]{1,0:T(8,128)(2,1)} %refs_6_.1, bf16[2048,4096]{1,0:T(8,128)(2,1)} %refs_6_.1), custom_call_target="tpu_custom_call" | custom-call | tf_op jit(solution)/shard_map/project/pallas_call | solution.py:305
  128.9 3.0 %collective-permute-done.6.one_ref.refs_1_ = bf16[2,512,256]{2,1,0:T(8,128)(2,1)} collective-permute-done((bf16[2,512,256]{2,1,0:T(8,128)(2,1)}, bf16[2,512,256]{2,1,0:T(8,128)(2,1)}, u32[]{:S(2)}, u32[]{:S(2)}) %collective-permute-start.6) | collective-permute-done | bytes 524320 | tf_op jit(solution)/shard_map/ppermute | solution.py:434
  131.9 10.2 %partials.3 = (bf16[2,1024,256]{2,1,0:T(8,128)(2,1)}, bf16[2,1024,256]{2,1,0:T(8,128)(2,1)}, bf16[2,1024,256]{2,1,0:T(8,128)(2,1)}, bf16[2,1024,256]{2,1,0:T(8,1...) custom-call(s32[20]{0:T(128)} %stack.90.table_ref, bf16[2048,512]{1,0:T(8,128)(2,1)} %get-tuple-element.34.own_ref, ...), custom_call_target="tpu_custom_call" | custom-call | tf_op jit(solution)/shard_map/partials/pallas_call | solution.py:379
  146.8 2.0 fusion.2
  149.3 9.9 %project.5.grad_ref = bf16[512,2048]{1,0:T(8,128)(2,1)} custom-call(s32[20]{0:T(128)} %stack.90.table_ref, bf16[3,512,256]{2,1,0:T(8,128)(2,1)} %collective-permute-done.20.refs_0_, bf16[2,512,256]{2,1,0:T(8,128)(2,1)} %collective-permute-done.6.one_ref.refs_1_, bf16[2,512,256]{2,1,0:T(8,128)(2,1)} %collective-permute-done.7.two_ref.refs_2_, ...), custom_call_target="tpu_custom_call" | custom-call | tf_op jit(solution)/shard_map/project/pallas_call | solution.py:305
  159.2 6.9 %pulls.1 = (bf16[512,2048]{1,0:T(8,128)(2,1)}, f32[256,1024]{1,0:T(8,128)}) custom-call(bf16[512,2048]{1,0:T(8,128)(2,1)} %project.5.grad_ref, bf16[512,256]{1,0:T(8,128)(2,1)} %bitcast.48, f32[32,512]{1,0:T(8,128)} %bitcast.53), custom_call_target="tpu_custom_call" | custom-call | tf_op jit(solution)/shard_map/pulls/pallas_call | solution.py:546
  168.5 2.0 fusion
  173.8 5.9 %collective-permute-done.19.y_last_ref = bf16[1024,256]{1,0:T(8,128)(2,1)} collective-permute-done((bf16[1024,256]{1,0:T(8,128)(2,1)}, bf16[1024,256]{1,0:T(8,128)(2,1)}, u32[]{:S(2)}, u32[]{:S(2)}) %collective-permute-start.19) | collective-permute-done | bytes 524320 | tf_op jit(solution)/shard_map/ppermute | solution.py:434
  180.3 2.8 %finish.2.refs_0_ = bf16[2,1024,512]{2,1,0:T(8,128)(2,1)} custom-call(bf16[2,1024,256]{2,1,0:T(8,128)(2,1)} %get-tuple-element.47.x_keep_ref, bf16[2,1024,256]{2,1,0:T(8,128)(2,1)} %collective-permute-done.16.x_got_ref, bf16[1024,256]{1,0:T(8,128)(2,1)} %collective-permute-done.17.x_last_ref, bf16[2,1024,256]{2,1,0:T(8,128)(2,1)} %get-tuple-element.48.y_keep_ref, ...), custom_call_target="tpu_custom_call" | custom-call | tf_op jit(solution)/shard_map/finish/pallas_call | solution.py:422
  183.1 7.9 %collective-permute-done.13.x_last_ref = bf16[1024,256]{1,0:T(8,128)(2,1)S(1)} collective-permute-done((bf16[1024,256]{1,0:T(8,128)(2,1)}, bf16[1024,256]{1,0:T(8,128)(2,1)S(1)}, u32[]{:S(2)}, u32[]{:S(2)}) %collective-permute-start.13) | collective-permute-done | bytes 524320 | tf_op jit(solution)/shard_map/ppermute | solution.py:434
  192.6 2.8 %finish.3 = bf16[2,1024,512]{2,1,0:T(8,128)(2,1)} custom-call(bf16[2,1024,256]{2,1,0:T(8,128)(2,1)} %get-tuple-element.43.x_keep_ref, bf16[2,1024,256]{2,1,0:T(8,128)(2,1)} %collective-permute-done.12.x_got_ref, bf16[1024,256]{1,0:T(8,128)(2,1)} %copy-done.11, bf16[2,1024,256]{2,1,0:T(8,128)(2,1)} %get-tuple-element.45.y_keep_ref, ...), custom_call_target="tpu_custom_call", output_to_operand_aliasing={{}: (6, {})} | custom-call | tf_op jit(solution)/shard_map/finish/pallas_call | solution.py:422
  196.4 9.8 %grads.1 = (bf16[512,2048]{1,0:T(8,128)(2,1)}, bf16[512,256]{1,0:T(8,128)(2,1)}, bf16[512,256]{1,0:T(8,128)(2,1)}) custom-call(bf16[512,2048]{1,0:T(8,128)(2,1)} %get-tuple-element.52.grad_ref, bf16[512,2048]{1,0:T(8,128)(2,1)} %get-tuple-element.32.scaled_ref, bf16[512,256]{1,0:T(8,128)(2,1)} %bitcast.46, bf16[512,256]{1,0:T(8,128)(2,1)} %bitcast.49, ...), custom_call_target="tpu_custom_call" | custom-call | tf_op jit(solution)/shard_map/grads/pallas_call | solution.py:548
  (65 shorter events, 26.8 us)
Async XLA Ops:
  1.9 2.0 collective-permute-start
  10.6 4.5 %collective-permute-start.1 = (f32[256,1024]{1,0:T(8,128)}, f32[256,1024]{1,0:T(8,128)S(1)}, u32[]{:S(2)}, u32[]{:S(2)}) collective-permute-start(f32[256,1024]{1,0:T(8,128)} %get-tuple-element.33), channel_id=1, source_target_pairs={{0,4},{1,5},{2,6},{3,7},{8,12},{9,13},{10,14},{11,15},{16,20},{17,... | collective-permute-start | bytes 3145736 | tf_op jit(solution)/shard_map/ppermute | solution.py:240
  23.8 43.5 %collective-permute-start.2 = (bf16[2048,512]{1,0:T(8,128)(2,1)}, bf16[2048,512]{1,0:T(8,128)(2,1)S(1)}, u32[]{:S(2)}, u32[]{:S(2)}) collective-permute-start(bf16[2048,512]{1,0:T(8,128)(2,1)} %get-tuple-element.34.own_ref), channel_id=1, source_target_pairs={{0,4},{4,0},{1,5},{5,1},{2,6},{6,2},{3,7},{7,3},{8,12},{12,8},{9,1... | collective-permute-start | bytes 6291464 | tf_op jit(solution)/shard_map/ppermute | solution.py:434
  25.3 26.3 %collective-permute-start.4 = (bf16[2,512,256]{2,1,0:T(8,128)(2,1)}, bf16[2,512,256]{2,1,0:T(8,128)(2,1)S(1)}, u32[]{:S(2)}, u32[]{:S(2)}) collective-permute-start(bf16[2,512,256]{2,1,0:T(8,128)(2,1)} %get-tuple-element.58.zero_ref), channel_id=1, source_target_pairs={{0,2},{1,3},{2,0},{3,1},{4,6},{5,7},{6,4},{7,5},{8,10},{9,11},{10,... | collective-permute-start | bytes 1572872 | tf_op jit(solution)/shard_map/ppermute | solution.py:434
  25.6 27.9 %collective-permute-start.8 = (bf16[2,512,256]{2,1,0:T(8,128)(2,1)}, bf16[2,512,256]{2,1,0:T(8,128)(2,1)S(1)}, u32[]{:S(2)}, u32[]{:S(2)}) collective-permute-start(bf16[2,512,256]{2,1,0:T(8,128)(2,1)} %get-tuple-element.58.zero_ref), channel_id=1, source_target_pairs={{0,1},{1,0},{2,3},{3,2},{4,5},{5,4},{6,7},{7,6},{8,9},{9,8},{10,11... | collective-permute-start | bytes 1572872 | tf_op jit(solution)/shard_map/ppermute | solution.py:434
  26.0 27.5 %collective-permute-start.3 = (bf16[2,512,256]{2,1,0:T(8,128)(2,1)}, bf16[2,512,256]{2,1,0:T(8,128)(2,1)}, u32[]{:S(2)}, u32[]{:S(2)}) collective-permute-start(bf16[2,512,256]{2,1,0:T(8,128)(2,1)} %get-tuple-element.58.zero_ref), channel_id=1, source_target_pairs={{1,2},{2,1},{5,6},{6,5},{9,10},{10,9},{13,14},{14,13},{17,18},{18,... | collective-permute-start | bytes 1572872 | tf_op jit(solution)/shard_map/ppermute | solution.py:452
  51.5 15.8 %copy-start.6 = (bf16[2,512,256]{2,1,0:T(8,128)(2,1)}, bf16[2,512,256]{2,1,0:T(8,128)(2,1)S(1)}, u32[]{:S(2)}) copy-start(bf16[2,512,256]{2,1,0:T(8,128)(2,1)S(1)} %collective-permute-done.4.two_ref.refs_2_) | copy-start | bytes 1572868
  51.5 15.8 %collective-permute-start.5 = (bf16[2,512,256]{2,1,0:T(8,128)(2,1)S(1)}, bf16[2,512,256]{2,1,0:T(8,128)(2,1)}, u32[]{:S(2)}, u32[]{:S(2)}) collective-permute-start(bf16[2,512,256]{2,1,0:T(8,128)(2,1)S(1)} %collective-permute-done.4.two_ref.refs_2_), channel_id=1, source_target_pairs={{1,0},{2,3},{5,4},{6,7},{9,8},{10,11},{13,12},{14,15},{17,16},{18,... | collective-permute-start | bytes 1572872 | tf_op jit(solution)/shard_map/ppermute | solution.py:451
  78.8 31.9 %collective-permute-start.11 = (bf16[3,512,256]{2,1,0:T(8,128)(2,1)}, bf16[3,512,256]{2,1,0:T(8,128)(2,1)S(1)}, u32[]{:S(2)}, u32[]{:S(2)}) collective-permute-start(bf16[3,512,256]{2,1,0:T(8,128)(2,1)} %get-tuple-element.40), channel_id=1, source_target_pairs={{0,4},{4,0},{1,5},{5,1},{2,6},{6,2},{3,7},{7,3},{8,12},{12,8},{9,1... | collective-permute-start | bytes 2359304 | tf_op jit(solution)/shard_map/ppermute | solution.py:434
  78.9 25.6 %collective-permute-start.7 = (bf16[2,512,256]{2,1,0:T(8,128)(2,1)}, bf16[2,512,256]{2,1,0:T(8,128)(2,1)}, u32[]{:S(2)}, u32[]{:S(2)}) collective-permute-start(bf16[2,512,256]{2,1,0:T(8,128)(2,1)} %get-tuple-element.38.zero_ref), channel_id=1, source_target_pairs={{0,2},{1,3},{2,0},{3,1},{4,6},{5,7},{6,4},{7,5},{8,10},{9,11},{10,... | collective-permute-start | bytes 1572872 | tf_op jit(solution)/shard_map/ppermute | solution.py:434
  79.0 65.3 %collective-permute-start.18 = (bf16[2,1024,256]{2,1,0:T(8,128)(2,1)}, bf16[2,1024,256]{2,1,0:T(8,128)(2,1)S(1)}, u32[]{:S(2)}, u32[]{:S(2)}) collective-permute-start(bf16[2,1024,256]{2,1,0:T(8,128)(2,1)} %get-tuple-element.49), channel_id=1, source_target_pairs={{0,16},{8,24},{16,0},{24,8},{1,17},{9,25},{17,1},{25,9},{2,18},{10... | collective-permute-start | bytes 3145736 | tf_op jit(solution)/shard_map/ppermute | solution.py:434
  104.6 24.3 %collective-permute-start.10 = (bf16[2,512,256]{2,1,0:T(8,128)(2,1)}, bf16[2,512,256]{2,1,0:T(8,128)(2,1)}, u32[]{:S(2)}, u32[]{:S(2)}) collective-permute-start(bf16[2,512,256]{2,1,0:T(8,128)(2,1)} %collective-permute-done.7.two_ref.refs_2_), channel_id=1, source_target_pairs={{1,0},{2,3},{5,4},{6,7},{9,8},{10,11},{13,12},{14,15},{17,16},{18,... | collective-permute-start | bytes 1572872 | tf_op jit(solution)/shard_map/ppermute | solution.py:451
  105.9 26.0 %collective-permute-start.6 = (bf16[2,512,256]{2,1,0:T(8,128)(2,1)}, bf16[2,512,256]{2,1,0:T(8,128)(2,1)}, u32[]{:S(2)}, u32[]{:S(2)}) collective-permute-start(bf16[2,512,256]{2,1,0:T(8,128)(2,1)} %get-tuple-element.38.zero_ref), channel_id=1, source_target_pairs={{0,1},{1,0},{2,3},{3,2},{4,5},{5,4},{6,7},{7,6},{8,9},{9,8},{10,11... | collective-permute-start | bytes 1572872 | tf_op jit(solution)/shard_map/ppermute | solution.py:434
  109.3 22.6 %collective-permute-start.9 = (bf16[2,512,256]{2,1,0:T(8,128)(2,1)}, bf16[2,512,256]{2,1,0:T(8,128)(2,1)}, u32[]{:S(2)}, u32[]{:S(2)}) collective-permute-start(bf16[2,512,256]{2,1,0:T(8,128)(2,1)} %get-tuple-element.38.zero_ref), channel_id=1, source_target_pairs={{1,2},{2,1},{5,6},{6,5},{9,10},{10,9},{13,14},{14,13},{17,18},{18,... | collective-permute-start | bytes 1572872 | tf_op jit(solution)/shard_map/ppermute | solution.py:452
  110.8 36.0 %collective-permute-start.16 = (bf16[2,1024,256]{2,1,0:T(8,128)(2,1)}, bf16[2,1024,256]{2,1,0:T(8,128)(2,1)}, u32[]{:S(2)}, u32[]{:S(2)}) collective-permute-start(bf16[2,1024,256]{2,1,0:T(8,128)(2,1)} %get-tuple-element.37), channel_id=1, source_target_pairs={{0,8},{8,0},{16,24},{24,16},{1,9},{9,1},{17,25},{25,17},{2,10},{10... | collective-permute-start | bytes 3145736 | tf_op jit(solution)/shard_map/ppermute | solution.py:434
  128.9 17.9 %copy-start.1 = (bf16[2,1024,256]{2,1,0:T(8,128)(2,1)S(1)}, bf16[2,1024,256]{2,1,0:T(8,128)(2,1)}, u32[]{:S(2)}) copy-start(bf16[2,1024,256]{2,1,0:T(8,128)(2,1)} %get-tuple-element.47.x_keep_ref) | copy-start | bytes 3145732
  142.1 26.4 %collective-permute-start.12 = (bf16[2,1024,256]{2,1,0:T(8,128)(2,1)}, bf16[2,1024,256]{2,1,0:T(8,128)(2,1)}, u32[]{:S(2)}, u32[]{:S(2)}) collective-permute-start(bf16[2,1024,256]{2,1,0:T(8,128)(2,1)} %get-tuple-element.44), channel_id=1, source_target_pairs={{0,8},{8,0},{16,24},{24,16},{1,9},{9,1},{17,25},{25,17},{2,10},{10... | collective-permute-start | bytes 3145736 | tf_op jit(solution)/shard_map/ppermute | solution.py:434
  142.7 6.6 %collective-permute-start.20 = (bf16[3,512,256]{2,1,0:T(8,128)(2,1)}, bf16[3,512,256]{2,1,0:T(8,128)(2,1)}, u32[]{:S(2)}, u32[]{:S(2)}) collective-permute-start(bf16[3,512,256]{2,1,0:T(8,128)(2,1)} %get-tuple-element.50), channel_id=1, source_target_pairs={{0,4},{4,0},{1,5},{5,1},{2,6},{6,2},{3,7},{7,3},{8,12},{12,8},{9,1... | collective-permute-start | bytes 2359304 | tf_op jit(solution)/shard_map/ppermute | solution.py:434
  142.7 29.3 %collective-permute-start.14 = (bf16[2,1024,256]{2,1,0:T(8,128)(2,1)}, bf16[2,1024,256]{2,1,0:T(8,128)(2,1)}, u32[]{:S(2)}, u32[]{:S(2)}) collective-permute-start(bf16[2,1024,256]{2,1,0:T(8,128)(2,1)} %get-tuple-element.46), channel_id=1, source_target_pairs={{0,16},{8,24},{16,0},{24,8},{1,17},{9,25},{17,1},{25,9},{2,18},{10... | collective-permute-start | bytes 3145736 | tf_op jit(solution)/shard_map/ppermute | solution.py:434
  145.3 34.4 %collective-permute-start.19 = (bf16[1024,256]{1,0:T(8,128)(2,1)}, bf16[1024,256]{1,0:T(8,128)(2,1)}, u32[]{:S(2)}, u32[]{:S(2)}) collective-permute-start(bf16[1024,256]{1,0:T(8,128)(2,1)} %fusion.3), channel_id=1, source_target_pairs={{0,8},{8,0},{16,24},{24,16},{1,9},{9,1},{17,25},{25,17},{2,10},{10... | collective-permute-start | bytes 1572872 | tf_op jit(solution)/shard_map/ppermute | solution.py:434
  148.8 31.5 %collective-permute-start.17 = (bf16[1024,256]{1,0:T(8,128)(2,1)}, bf16[1024,256]{1,0:T(8,128)(2,1)}, u32[]{:S(2)}, u32[]{:S(2)}) collective-permute-start(bf16[1024,256]{1,0:T(8,128)(2,1)} %fusion.2), channel_id=1, source_target_pairs={{0,16},{8,24},{16,0},{24,8},{1,17},{9,25},{17,1},{25,9},{2,18},{10... | collective-permute-start | bytes 1572872 | tf_op jit(solution)/shard_map/ppermute | solution.py:434
  166.1 29.3 %collective-permute-start.21 = (f32[256,1024]{1,0:T(8,128)}, f32[256,1024]{1,0:T(8,128)S(1)}, u32[]{:S(2)}, u32[]{:S(2)}) collective-permute-start(f32[256,1024]{1,0:T(8,128)} %get-tuple-element.54), channel_id=1, source_target_pairs={{4,0},{5,1},{6,2},{7,3},{12,8},{13,9},{14,10},{15,11},{20,16},{21,... | collective-permute-start | bytes 3145736 | tf_op jit(solution)/shard_map/ppermute | solution.py:240
  170.5 20.5 %collective-permute-start.13 = (bf16[1024,256]{1,0:T(8,128)(2,1)}, bf16[1024,256]{1,0:T(8,128)(2,1)S(1)}, u32[]{:S(2)}, u32[]{:S(2)}) collective-permute-start(bf16[1024,256]{1,0:T(8,128)(2,1)} %fusion), channel_id=1, source_target_pairs={{0,16},{8,24},{16,0},{24,8},{1,17},{9,25},{17,1},{25,9},{2,18},{10... | collective-permute-start | bytes 1572872 | tf_op jit(solution)/shard_map/ppermute | solution.py:434
  173.2 17.8 %collective-permute-start.15 = (bf16[1024,256]{1,0:T(8,128)(2,1)S(1)}, bf16[1024,256]{1,0:T(8,128)(2,1)S(1)}, u32[]{:S(2)}, u32[]{:S(2)}) collective-permute-start(bf16[1024,256]{1,0:T(8,128)(2,1)S(1)} %fusion.1), channel_id=1, source_target_pairs={{0,8},{8,0},{16,24},{24,16},{1,9},{9,1},{17,25},{25,17},{2,10},{10... | collective-permute-start | bytes 1572872 | tf_op jit(solution)/shard_map/ppermute | solution.py:434
  (11 other events, 80.8 us)
